TPU v7x, 256 devices: a whole 4x4x8 slice. The times are simulated.
256 devices in a mesh: seq: 256 (over y, z, x, core).
Axes of the slice: x: 4, y: 4, z: 8, core: 2. Of those that a mesh axis runs over, the one named last changes fastest.
Arguments:
- saved_input: bfloat16 [65536, 192], P('seq'), may hold values from -6 to 6
- cotangent: bfloat16 [65536, 192], P('seq'), may hold values from -15 to 15
- w_in: bfloat16 [384, 768], replicated, may hold values from -0.3125 to 0.3125
- bias_in: float32 [768], replicated, may hold values from -4 to 4
- w_out: bfloat16 [768, 384], replicated, may hold values from -0.21875 to 0.21875
- residual_logit: float32 [384], replicated, may hold values from -1 to 2
- branch_scale: float32 [384], replicated, may hold values from 0.1 to 1
Outputs:
- grad_input: bfloat16 [65536, 192], P('seq')
- grad_w_in: float32 [384, 768], replicated
- grad_w_out: float32 [768, 384], replicated
All inputs are finite; a program needn't handle non-finite values.
Results may differ from a plain program's by a relative error of at most 0.02.
Values may be sent and summed in bfloat16 or wider, within the bound.
A program may use at most 64 MiB of HBM per device.

v0:
```python
import functools

import jax
import jax.numpy as jnp
from jax import lax
from jax.experimental import pallas as pl
from jax.experimental.pallas import tpu as pltpu
from jax.sharding import PartitionSpec as P

epsilon = 1e-05
tanh_scale = 0.7978845608028654
cubic_coef = 0.044715
LANES = 128
PAD = 256
F32 = jnp.float32
BF16 = jnp.bfloat16


def row_dot(left, right):
    return jnp.dot(left, right, preferred_element_type=F32)


def column_dot(left, right):
    return lax.dot_general(left, right, (((0,), (0,)), ((), ())), preferred_element_type=F32)


def lanes_below(rows, lanes, bound):
    return lax.broadcasted_iota(jnp.int32, (rows, lanes), 1) < bound


def widen(values, width):
    rows = values.shape[0]
    keep = lanes_below(rows, PAD, width)
    first = jnp.where(keep, values[:, :PAD], 0.0)
    second = pltpu.roll(values[:, 2 * width - PAD :], width, 1)
    return jnp.concatenate([first, jnp.where(keep, second, 0.0)], axis=1)


def narrow(first, second, width):
    moved = pltpu.roll(second, width - LANES, 1)
    return jnp.concatenate([first[:, :LANES], first[:, LANES:] + moved[:, :LANES], moved[:, LANES:]], axis=1)


def halves(state, block):
    rows = state.shape[0]
    view = state.reshape(rows // (2 * block), 2, block, PAD)
    return view[:, 0].reshape(rows // 2, PAD), view[:, 1].reshape(rows // 2, PAD)


def unite(first, second, block):
    rows = first.shape[0]
    parts = [h.reshape(rows // block, 1, block, PAD) for h in (first, second)]
    return jnp.concatenate(parts, axis=1).reshape(2 * rows, PAD)


def kernel(
    dims, scale_out,
    x_ref, ct_ref, win_ref, bias_ref, wout_ref, logit_ref, scale_ref,
    gx_ref, grads_ref,
    ra, tb, rb, flat, wi, wit, wo, wot, gate, scale,
    nrm, inv, slope, nlc, act, pg, bgc,
    gb, rc, hsum, rd, rz, rg, tx, rx1, tx2, rx2,
    a_send, a_recv, b_send, b_recv, c_send, c_recv, d_send, d_recv, z_send, z_recv,
    e_send, e_recv, f_send, f_recv, u_send, u_recv, v_send, v_recv,
):
    ny, nz, nx, nc = dims
    nq, ns, npl = ny * nz, nx * nc, ny * nx
    rows, pairs = nq * ns, nq * ns // 2
    width = x_ref.shape[2]
    low_levels = ns.bit_length() - 1
    levels = rows.bit_length() - 1
    me = lax.axis_index("seq")
    q, s = me // ns, me % ns
    y, z, xc, c = q // nz, q % nz, s // nc, s % nc
    plane = y * nx + xc

    def id_qs(qq, ss):
        return qq * ns + ss

    def id_plane(pp):
        return (((pp // nx) * nz + z) * nx + pp % nx) * nc + c

    def id_z(zz):
        return ((y * nz + zz) * nx + xc) * nc + c

    sibling = id_qs(q, xc * nc + (1 - c))

    barrier = pltpu.get_barrier_semaphore()

    def greet(device):
        pl.semaphore_signal(barrier, inc=1, device_id=(device,), device_id_type=pl.DeviceIdType.MESH)

    @pl.loop(1, nq)
    def _(j):
        greet(id_qs((q + j) % nq, s))

    @pl.loop(1, ns)
    def _(j):
        greet(id_qs(q, (s + j) % ns))

    for jy in range(1, ny):
        for jx in range(1, nx):
            greet(id_plane(((y + jy) % ny) * nx + (xc + jx) % nx))
    pl.semaphore_wait(barrier, (nq - 1) + (ns - 1) + (ny - 1) * (nx - 1))

    def send(src, dst, send_sem, recv_sem, device):
        return pltpu.make_async_remote_copy(
            src_ref=src, dst_ref=dst, send_sem=send_sem, recv_sem=recv_sem,
            device_id=(device,), device_id_type=pl.DeviceIdType.MESH,
        )

    def exchange(count, place, src, dst, send_sem, recv_sem, device_of):
        def copy(j):
            to = (place + j) % count
            return send(src.at[to], dst.at[place], send_sem.at[j - 1], recv_sem.at[j - 1], device_of(to))

        def start():
            @pl.loop(1, count)
            def _(j):
                copy(j).start()

        def wait():
            @pl.loop(1, count)
            def _(j):
                copy(j).wait()

        return start, wait

    def start_a(k, src):
        start, wait = exchange(nq, q, src, ra.at[k], a_send.at[k], a_recv.at[k], lambda i: id_qs(i, s))
        start()
        ra[k, q] = src[q]
        return wait

    def put_rows(block):
        values = block.astype(F32).reshape(rows, width)
        flat[0] = values[:, :LANES]
        flat[1, :, : width - LANES] = values[:, LANES:]

    def strided(start, size, stride):
        return jnp.concatenate([flat[h, pl.ds(start, size, stride=stride), :] for h in range(2)], axis=1)

    def start_b(k):
        put_rows(ra[k])
        for r in range(ns):
            tb[k, r] = strided(r, nq, ns)[:, :width].astype(BF16)
        start, wait = exchange(ns, s, tb.at[k], rb.at[k], b_send.at[k], b_recv.at[k], lambda i: id_qs(q, i))
        start()
        rb[k, s] = tb[k, s]
        return wait

    flat[...] = jnp.zeros_like(flat)
    wait_a0 = start_a(0, x_ref)

    wide_in = jnp.zeros((PAD - width, win_ref.shape[1]), BF16)
    wi[:width] = win_ref[:width]
    wi[width:PAD] = wide_in
    wi[PAD : PAD + width] = win_ref[width:]
    wi[PAD + width :] = wide_in
    wit[...] = wi[...].T
    wo[...] = widen(wout_ref[...].astype(F32), width).astype(BF16)
    wot[...] = wo[...].T
    gate[...] = jax.nn.sigmoid(widen(jnp.broadcast_to(logit_ref[...], (8, 2 * width)), width))
    scale[...] = widen(jnp.broadcast_to(scale_ref[...], (8, 2 * width)), width)
    lane = lax.broadcasted_iota(jnp.int32, (1, 2 * PAD), 1) % PAD
    mask = jnp.where(lane < width, 1.0, 0.0)

    wait_a0()
    wait_b0 = start_b(0)
    wait_a1 = start_a(1, ct_ref)
    wait_b0()

    def load_state(k):
        put_rows(rb[k])
        return jnp.concatenate([flat[0], flat[1]], axis=1)

    def swap_order(state, major, minor):
        flat[0] = state[:, :LANES]
        flat[1] = state[:, LANES:]
        return jnp.concatenate([strided(j, major, minor) for j in range(minor)], axis=0)

    def block_of(level):
        return nq * 2**level if level < low_levels else 2**level

    state = load_state(0)
    for level in range(levels):
        if level == low_levels:
            state = swap_order(state, ns, nq)
            wait_a1()
            wait_b1 = start_b(1)
        first, second = halves(state, block_of(level))
        paired = jnp.concatenate([first, second], axis=1)
        average = jnp.sum(paired, axis=1, keepdims=True) * (1.0 / (2 * width))
        centered = paired - average * mask
        inverse = lax.rsqrt(jnp.sum(centered * centered, axis=1, keepdims=True) * (1.0 / (2 * width)) + epsilon)
        normed = centered * inverse
        nrm[level] = normed
        inv[level] = inverse
        here = pl.ds(level * pairs, pairs)
        nlc[here, :] = narrow(normed[:, :PAD], normed[:, PAD:], width).astype(BF16)
        preact = row_dot(normed.astype(BF16), wi[...]) + bias_ref[...]
        square = preact * preact
        tangent = jnp.tanh(preact * (tanh_scale + (tanh_scale * cubic_coef) * square))
        half = 0.5 + 0.5 * tangent
        activated = (preact * half).astype(BF16)
        act[here, :] = activated
        slope[level] = half + (0.5 * preact) * (1.0 - tangent * tangent) * (
            tanh_scale + (3.0 * tanh_scale * cubic_coef) * square
        )
        if level + 1 < levels:
            result = gate[0:1] * paired + scale[0:1] * row_dot(activated, wo[...])
            state = unite(result[:, :PAD], result[:, PAD:], block_of(level))

    wait_b1()
    state = swap_order(load_state(1), ns, nq)
    for level in reversed(range(levels)):
        if level == low_levels - 1:
            state = swap_order(state, nq, ns)
        first, second = halves(state, block_of(level))
        upstream = jnp.concatenate([first, second], axis=1)
        branch = scale[0:1] * upstream
        here = pl.ds(level * pairs, pairs)
        bgc[here, :] = narrow(branch[:, :PAD], branch[:, PAD:], width).astype(BF16)
        preact_grad = (row_dot(branch.astype(BF16), wot[...]) * slope[level]).astype(BF16)
        pg[here, :] = preact_grad
        normed_grad = row_dot(preact_grad, wit[...])
        normed = nrm[level]
        mean_grad = jnp.sum(normed_grad, axis=1, keepdims=True) * (1.0 / (2 * width))
        mean_both = jnp.sum(normed_grad * normed, axis=1, keepdims=True) * (1.0 / (2 * width))
        grad = gate[0:1] * upstream + inv[level] * (normed_grad - mean_grad * mask - normed * mean_both)
        state = unite(grad[:, :PAD], grad[:, PAD:], block_of(level))

    tx[...] = state[:, :width].reshape(ns, nq, width).astype(BF16)
    start_u, wait_u = exchange(ns, s, tx, rx1, u_send, u_recv, lambda i: id_qs(q, i))
    start_u()
    rx1[s] = tx[s]

    units = act.shape[1]
    piece = gb.shape[2]
    span = 2 * width
    count = span // piece
    for h in range(units // span):
        block = pl.ds(h * span, span)
        grad_in = column_dot(nlc[...], pg[:, block])
        gb[0, pl.ds(h * count, count)] = grad_in.reshape(count, piece, span).astype(BF16)
    for h in range(units // span):
        block = pl.ds(h * span, span)
        grad_out = column_dot(act[:, block], bgc[...])
        gb[1, pl.ds(h * count, count)] = grad_out.reshape(count, piece, span).astype(BF16)

    copy_c = send(gb.at[1 - c], rc, c_send, c_recv, sibling)
    copy_c.start()

    wait_u()
    put_rows(rx1[...])
    for j in range(nq):
        tx2[j] = strided(j, ns, nq)[:, :width].astype(BF16)
    start_v, wait_v = exchange(nq, q, tx2, rx2, v_send, v_recv, lambda i: id_qs(i, s))
    start_v()
    rx2[q] = tx2[q]

    copy_c.wait()
    hsum[...] = (gb[c].astype(F32) + rc[...].astype(F32)).astype(BF16)

    start_d, wait_d = exchange(npl, plane, hsum, rd, d_send, d_recv, id_plane)
    start_d()
    rd[plane] = hsum[plane]
    wait_d()
    total = rd[0].astype(F32)
    for i in range(1, npl):
        total = total + rd[i].astype(F32)
    rz[z] = total.astype(BF16)

    def copy_z(j):
        return send(rz.at[z], rz.at[z], z_send.at[j - 1], z_recv.at[j - 1], id_z((z + j) % nz))

    @pl.loop(1, nz)
    def _(j):
        copy_z(j).start()

    @pl.loop(1, nz)
    def _(j):
        copy_z(j).wait()

    total = rz[0].astype(F32)
    for i in range(1, nz):
        total = total + rz[i].astype(F32)
    rg[c, plane] = (total * scale_out).astype(BF16)

    def copy_e(j):
        mine = rg.at[c, plane]
        return send(mine, mine, e_send.at[j - 1], e_recv.at[j - 1], id_plane((plane + j) % npl))

    @pl.loop(1, npl)
    def _(j):
        copy_e(j).start()

    @pl.loop(1, npl)
    def _(j):
        copy_e(j).wait()

    copy_f = send(rg.at[c], rg.at[c], f_send, f_recv, sibling)
    copy_f.start()
    wait_v()
    gx_ref[...] = rx2[...]
    copy_f.wait()
    grads_ref[...] = rg[...]


def build(mesh, dims, interpret=False):
    ny, nz, nx, nc = dims
    nq, ns, npl = ny * nz, nx * nc, ny * nx
    rows, pairs = nq * ns, nq * ns // 2
    levels = rows.bit_length() - 1

    def step(saved_input, cotangent, w_in, bias_in, w_out, residual_logit, branch_scale):
        width, units = saved_input.shape[1], w_in.shape[1]
        piece = units // npl
        span = 2 * width
        vmem = pltpu.VMEM
        dma = pltpu.SemaphoreType.DMA
        scratch = [
            vmem((2, nq, ns, width), BF16),
            vmem((2, ns, nq, width), BF16),
            vmem((2, ns, nq, width), BF16),
            vmem((2, rows, LANES), F32),
            vmem((2 * PAD, units), BF16),
            vmem((units, 2 * PAD), BF16),
            vmem((units, 2 * PAD), BF16),
            vmem((2 * PAD, units), BF16),
            vmem((8, 2 * PAD), F32),
            vmem((8, 2 * PAD), F32),
            vmem((levels, pairs, 2 * PAD), F32),
            vmem((levels, pairs, 1), F32),
            vmem((levels, pairs, units), F32),
            vmem((levels * pairs, span), BF16),
            vmem((levels * pairs, units), BF16),
            vmem((levels * pairs, units), BF16),
            vmem((levels * pairs, span), BF16),
            vmem((2, npl, piece, span), BF16),
            vmem((npl, piece, span), BF16),
            vmem((npl, piece, span), BF16),
            vmem((npl, piece, span), BF16),
            vmem((nz, piece, span), BF16),
            vmem((2, npl, piece, span), BF16),
            vmem((ns, nq, width), BF16),
            vmem((ns, nq, width), BF16),
            vmem((nq, ns, width), BF16),
            vmem((nq, ns, width), BF16),
            dma((2, nq - 1)), dma((2, nq - 1)),
            dma((2, ns - 1)), dma((2, ns - 1)),
            dma, dma,
            dma((npl - 1,)), dma((npl - 1,)),
            dma((nz - 1,)), dma((nz - 1,)),
            dma((npl - 1,)), dma((npl - 1,)),
            dma, dma,
            dma((ns - 1,)), dma((ns - 1,)),
            dma((nq - 1,)), dma((nq - 1,)),
        ]
        in_vmem = pl.BlockSpec(memory_space=pltpu.VMEM)
        gx, grads = pl.pallas_call(
            functools.partial(kernel, dims, float(rows * rows) ** (-0.5)),
            out_shape=(
                jax.ShapeDtypeStruct((nq, ns, width), BF16),
                jax.ShapeDtypeStruct((2, npl, piece, span), BF16),
            ),
            in_specs=[in_vmem] * 7,
            out_specs=(in_vmem, in_vmem),
            scratch_shapes=scratch,
            compiler_params=pltpu.CompilerParams(collective_id=0, has_side_effects=True, vmem_limit_bytes=60 * 2**20),
        )(
            saved_input.reshape(nq, ns, width), cotangent.reshape(nq, ns, width), w_in, bias_in.reshape(1, units),
            w_out, residual_logit.reshape(1, span), branch_scale.reshape(1, span),
        )
        parts = grads.reshape(2, units // span, span, span).astype(F32)
        grad_in = parts[0].transpose(1, 0, 2).reshape(span, units)
        grad_out = parts[1].reshape(units, span)
        return gx.reshape(rows, width), grad_in, grad_out

    in_specs = (P("seq", None), P("seq", None), P(), P(), P(), P(), P())
    out_specs = (P("seq", None), P(), P())
    return jax.shard_map(step, mesh=mesh, in_specs=in_specs, out_specs=out_specs, check_vma=False)


def solution(mesh):
    return build(mesh, (4, 8, 4, 2))
```

profile of v0, /device:TPU:1, one launch (start us, length us, event | category | flops | bytes accessed | tf_op | source)
XLA Modules:
  0.0 85.0 jit_solution(3815142332626293226)
XLA Ops:
  0.6 1.3 %reshape.36.logit_ref = f32[1,384]{1,0:T(1,128)} reshape(f32[384]{0:T(512)} %param.12) | data formatting | bytes 3072 | tf_op jit(solution)/shard_map/reshape | solution.py:373
  1.9 1.3 %reshape.37.scale_ref = f32[1,384]{1,0:T(1,128)} reshape(f32[384]{0:T(512)} %param.13) | data formatting | bytes 3072 | tf_op jit(solution)/shard_map/reshape | solution.py:373
  3.2 1.3 %reshape.35.bias_ref = f32[1,768]{1,0:T(1,128)} reshape(f32[768]{0:T(1024)} %param.10) | data formatting | bytes 6144 | tf_op jit(solution)/shard_map/reshape | solution.py:372
  4.4 1.7 %copy.10 = bf16[256,192]{1,0:T(8,128)(2,1)} copy(bf16[256,192]{0,1:T(8,128)(2,1)} %param.7) | data formatting | bytes 196608 | tf_op args[0]
  6.1 1.7 %copy.11 = bf16[256,192]{1,0:T(8,128)(2,1)} copy(bf16[256,192]{0,1:T(8,128)(2,1)} %param.8) | data formatting | bytes 196608 | tf_op args[1]
  7.7 72.1 %shard_map.94 = (bf16[32,8,192]{2,1,0:T(8,128)(2,1)}, bf16[2,16,48,384]{3,2,1,0:T(8,128)(2,1)}) custom-call(bf16[32,8,192]{2,1,0:T(8,128)(2,1)} %bitcast.12, bf16[32,8,192]{2,1,0:T(8,128)(2,1)} %bitcast.13, bf16[384,768]{1,0:T(8,128)(2,1)} %win_ref.1, f32[1,768]{1,0:T(1,128)} %reshape.35.bias_ref, bf16[768,384]{1,0:T(8,128)(2,1)} %wout_ref.1, ...), custom_call_target="tpu_custom_call" | custom-call | tf_op jit(solution)/shard_map/pallas_call | solution.py:361
  79.8 1.6 %copy.13 = bf16[256,192]{0,1:T(8,128)(2,1)} copy(bf16[256,192]{1,0:T(8,128)(2,1)} %bitcast.14) | data formatting | bytes 196608
  81.4 2.4 %fusion = (f32[1,16,48,384]{3,2,1,0:T(8,128)}, f32[1,16,48,384]{3,2,1,0:T(8,128)S(1)}) fusion(bf16[2,16,48,384]{3,2,1,0:T(8,128)(2,1)} %get-tuple-element.6), kind=kLoop, calls=%fused_computation | loop fusion | bytes 4718592 | tf_op jit(solution)/shard_map/slice | solution.py:377
  83.9 1.1 %copy.14 = f32[2,48,8,384]{3,2,0,1:T(8,128)} copy(f32[2,48,8,384]{3,2,1,0:T(8,128)S(1)} %bitcast.9) | data formatting | bytes 2359296 | tf_op jit(solution)/shard_map/reshape | solution.py:376
where the time goes:
time: 85.2 us; the launch traced here: 85 us
  Pallas kernels  72.1 us (85%)
  local copies, waits for them, and re-layouts  12.3 us (14%)
    pallas_call x1, Pallas kernels, step(): pl.pallas_call(functools.partial(kernel, dims, float(rows * rows) ** (-0....  72.1 us
    unnamed x3, local copies, waits for them, and re-layouts  4.95 us
    slice x1, local copies, waits for them, and re-layouts, step(): grad_out = parts[1].reshape(units, span)  2.41 us

commit v1 on v0

--- a/solution.py
+++ b/solution.py
@@ -55,18 +55,19 @@
 
 def kernel(
     dims, scale_out,
-    x_ref, ct_ref, win_ref, bias_ref, wout_ref, logit_ref, scale_ref,
+    xt_hbm, ct_hbm, win_hbm, bias_hbm, wout_hbm, logit_hbm, scale_hbm,
     gx_ref, grads_ref,
+    xt, win, bias_row, wout, logit_row, scale_row, xs,
     ra, tb, rb, flat, wi, wit, wo, wot, gate, scale,
     nrm, inv, slope, nlc, act, pg, bgc,
     gb, rc, hsum, rd, rz, rg, tx, rx1, tx2, rx2,
-    a_send, a_recv, b_send, b_recv, c_send, c_recv, d_send, d_recv, z_send, z_recv,
+    load_sem, a_send, a_recv, b_send, b_recv, c_send, c_recv, d_send, d_recv, z_send, z_recv,
     e_send, e_recv, f_send, f_recv, u_send, u_recv, v_send, v_recv,
 ):
     ny, nz, nx, nc = dims
     nq, ns, npl = ny * nz, nx * nc, ny * nx
     rows, pairs = nq * ns, nq * ns // 2
-    width = x_ref.shape[2]
+    width = xt.shape[1]
     low_levels = ns.bit_length() - 1
     levels = rows.bit_length() - 1
     me = lax.axis_index("seq")
@@ -101,6 +102,34 @@
     for jy in range(1, ny):
         for jx in range(1, nx):
             greet(id_plane(((y + jy) % ny) * nx + (xc + jx) % nx))
+
+    operands = (
+        (xt_hbm, xt.at[0]), (ct_hbm, xt.at[1]), (logit_hbm, logit_row), (scale_hbm, scale_row), (bias_hbm, bias_row),
+        (win_hbm, win), (wout_hbm, wout),
+    )
+    loads = [pltpu.make_async_copy(src, dst, load_sem.at[i]) for i, (src, dst) in enumerate(operands)]
+    for load in loads:
+        load.start()
+    flat[...] = jnp.zeros_like(flat)
+    for k in range(2):
+        loads[k].wait()
+        xs[k] = xt[k].T.reshape(nq, ns, width)
+    for load in loads[2:]:
+        load.wait()
+    wide_in = jnp.zeros((PAD - width, win.shape[1]), BF16)
+    wi[:width] = win[:width]
+    wi[width:PAD] = wide_in
+    wi[PAD : PAD + width] = win[width:]
+    wi[PAD + width :] = wide_in
+    wit[...] = wi[...].T
+    wo[...] = widen(wout[...].astype(F32), width).astype(BF16)
+    wot[...] = wo[...].T
+    gate[...] = jax.nn.sigmoid(widen(jnp.broadcast_to(logit_row[...].reshape(1, 2 * width), (8, 2 * width)), width))
+    scale[...] = widen(jnp.broadcast_to(scale_row[...].reshape(1, 2 * width), (8, 2 * width)), width)
+    bias = bias_row[...].reshape(1, bias_row.shape[0])
+    lane = lax.broadcasted_iota(jnp.int32, (1, 2 * PAD), 1) % PAD
+    mask = jnp.where(lane < width, 1.0, 0.0)
+
     pl.semaphore_wait(barrier, (nq - 1) + (ns - 1) + (ny - 1) * (nx - 1))
 
     def send(src, dst, send_sem, recv_sem, device):
@@ -109,27 +138,37 @@
             device_id=(device,), device_id_type=pl.DeviceIdType.MESH,
         )
 
+    def each(count, copy):
+        def start():
+            @pl.loop(1, count)
+            def _(j):
+                copy(j).start()
+
+        def wait():
+            @pl.loop(1, count)
+            def _(j):
+                copy(j).wait()
+
+        return start, wait
+
     def exchange(count, place, src, dst, send_sem, recv_sem, device_of):
         def copy(j):
             to = (place + j) % count
             return send(src.at[to], dst.at[place], send_sem.at[j - 1], recv_sem.at[j - 1], device_of(to))
 
-        def start():
-            @pl.loop(1, count)
-            def _(j):
-                copy(j).start()
-
-        def wait():
-            @pl.loop(1, count)
-            def _(j):
-                copy(j).wait()
-
-        return start, wait
-
-    def start_a(k, src):
-        start, wait = exchange(nq, q, src, ra.at[k], a_send.at[k], a_recv.at[k], lambda i: id_qs(i, s))
+        return each(count, copy)
+
+    def spread(count, place, ref, send_sem, recv_sem, device_of):
+        def copy(j):
+            to = (place + j) % count
+            return send(ref.at[place], ref.at[place], send_sem.at[j - 1], recv_sem.at[j - 1], device_of(to))
+
+        return each(count, copy)
+
+    def start_a(k):
+        start, wait = exchange(nq, q, xs.at[k], ra.at[k], a_send.at[k], a_recv.at[k], lambda i: id_qs(i, s))
         start()
-        ra[k, q] = src[q]
+        ra[k, q] = xs[k, q]
         return wait
 
     def put_rows(block):
@@ -149,25 +188,12 @@
         rb[k, s] = tb[k, s]
         return wait
 
-    flat[...] = jnp.zeros_like(flat)
-    wait_a0 = start_a(0, x_ref)
-
-    wide_in = jnp.zeros((PAD - width, win_ref.shape[1]), BF16)
-    wi[:width] = win_ref[:width]
-    wi[width:PAD] = wide_in
-    wi[PAD : PAD + width] = win_ref[width:]
-    wi[PAD + width :] = wide_in
-    wit[...] = wi[...].T
-    wo[...] = widen(wout_ref[...].astype(F32), width).astype(BF16)
-    wot[...] = wo[...].T
-    gate[...] = jax.nn.sigmoid(widen(jnp.broadcast_to(logit_ref[...], (8, 2 * width)), width))
-    scale[...] = widen(jnp.broadcast_to(scale_ref[...], (8, 2 * width)), width)
-    lane = lax.broadcasted_iota(jnp.int32, (1, 2 * PAD), 1) % PAD
-    mask = jnp.where(lane < width, 1.0, 0.0)
-
+    wait_a0 = start_a(0)
+    wait_a1 = start_a(1)
     wait_a0()
     wait_b0 = start_b(0)
-    wait_a1 = start_a(1, ct_ref)
+    wait_a1()
+    wait_b1 = start_b(1)
     wait_b0()
 
     def load_state(k):
@@ -186,8 +212,6 @@
     for level in range(levels):
         if level == low_levels:
             state = swap_order(state, ns, nq)
-            wait_a1()
-            wait_b1 = start_b(1)
         first, second = halves(state, block_of(level))
         paired = jnp.concatenate([first, second], axis=1)
         average = jnp.sum(paired, axis=1, keepdims=True) * (1.0 / (2 * width))
@@ -198,7 +222,7 @@
         inv[level] = inverse
         here = pl.ds(level * pairs, pairs)
         nlc[here, :] = narrow(normed[:, :PAD], normed[:, PAD:], width).astype(BF16)
-        preact = row_dot(normed.astype(BF16), wi[...]) + bias_ref[...]
+        preact = row_dot(normed.astype(BF16), wi[...]) + bias
         square = preact * preact
         tangent = jnp.tanh(preact * (tanh_scale + (tanh_scale * cubic_coef) * square))
         half = 0.5 + 0.5 * tangent
@@ -235,21 +259,28 @@
     start_u()
     rx1[s] = tx[s]
 
+    chunks = gb.shape[1]
+    span = 2 * width
     units = act.shape[1]
-    piece = gb.shape[2]
-    span = 2 * width
-    count = span // piece
-    for h in range(units // span):
-        block = pl.ds(h * span, span)
-        grad_in = column_dot(nlc[...], pg[:, block])
-        gb[0, pl.ds(h * count, count)] = grad_in.reshape(count, piece, span).astype(BF16)
-    for h in range(units // span):
-        block = pl.ds(h * span, span)
-        grad_out = column_dot(act[:, block], bgc[...])
-        gb[1, pl.ds(h * count, count)] = grad_out.reshape(count, piece, span).astype(BF16)
-
-    copy_c = send(gb.at[1 - c], rc, c_send, c_recv, sibling)
-    copy_c.start()
+    in_rows, out_rows = span // chunks, units // chunks
+    to_sibling = []
+    for k in range(chunks):
+        grad_in = column_dot(nlc[:, k * in_rows : (k + 1) * in_rows], pg[...])
+        for h in range(2):
+            gb[0, k, :, h] = grad_in[:, h * span : (h + 1) * span].reshape(npl, 8, span).astype(BF16)
+        grad_out = column_dot(act[:, k * out_rows : (k + 1) * out_rows], bgc[...])
+        gb[1, k] = grad_out.reshape(npl, 2, 8, span).astype(BF16)
+        to_sibling.append(send(gb.at[1 - c, k], rc.at[k], c_send.at[k], c_recv.at[k], sibling))
+        to_sibling[k].start()
+
+    plane_waits = []
+    for k in range(chunks):
+        to_sibling[k].wait()
+        hsum[k] = (gb[c, k].astype(F32) + rc[k].astype(F32)).astype(BF16)
+        start, wait = exchange(npl, plane, hsum.at[k], rd.at[k], d_send.at[k], d_recv.at[k], id_plane)
+        start()
+        plane_waits.append(wait)
+        rd[k, plane] = hsum[k, plane]
 
     wait_u()
     put_rows(rx1[...])
@@ -259,55 +290,52 @@
     start_v()
     rx2[q] = tx2[q]
 
-    copy_c.wait()
-    hsum[...] = (gb[c].astype(F32) + rc[...].astype(F32)).astype(BF16)
-
-    start_d, wait_d = exchange(npl, plane, hsum, rd, d_send, d_recv, id_plane)
-    start_d()
-    rd[plane] = hsum[plane]
-    wait_d()
-    total = rd[0].astype(F32)
-    for i in range(1, npl):
-        total = total + rd[i].astype(F32)
-    rz[z] = total.astype(BF16)
-
-    def copy_z(j):
-        return send(rz.at[z], rz.at[z], z_send.at[j - 1], z_recv.at[j - 1], id_z((z + j) % nz))
-
-    @pl.loop(1, nz)
-    def _(j):
-        copy_z(j).start()
-
-    @pl.loop(1, nz)
-    def _(j):
-        copy_z(j).wait()
-
-    total = rz[0].astype(F32)
-    for i in range(1, nz):
-        total = total + rz[i].astype(F32)
-    rg[c, plane] = (total * scale_out).astype(BF16)
-
-    def copy_e(j):
-        mine = rg.at[c, plane]
-        return send(mine, mine, e_send.at[j - 1], e_recv.at[j - 1], id_plane((plane + j) % npl))
-
-    @pl.loop(1, npl)
-    def _(j):
-        copy_e(j).start()
-
-    @pl.loop(1, npl)
-    def _(j):
-        copy_e(j).wait()
-
-    copy_f = send(rg.at[c], rg.at[c], f_send, f_recv, sibling)
-    copy_f.start()
+    def added(ref, count):
+        total = ref[0].astype(F32)
+        for i in range(1, count):
+            total = total + ref[i].astype(F32)
+        return total
+
+    z_waits = []
+    for k in range(chunks):
+        plane_waits[k]()
+        rz[k, z] = added(rd.at[k], npl).astype(BF16)
+        start, wait = spread(nz, z, rz.at[k], z_send.at[k], z_recv.at[k], id_z)
+        start()
+        z_waits.append(wait)
+
+    gather_waits = []
+    for k in range(chunks):
+        z_waits[k]()
+        rg[c, k, plane] = (added(rz.at[k], nz) * scale_out).astype(BF16)
+        start, wait = spread(npl, plane, rg.at[c, k], e_send.at[k], e_recv.at[k], id_plane)
+        start()
+        gather_waits.append(wait)
+    over = []
+    for k in range(chunks):
+        gather_waits[k]()
+        over.append(send(rg.at[c, k], rg.at[c, k], f_send.at[k], f_recv.at[k], sibling))
+        over[k].start()
     wait_v()
     gx_ref[...] = rx2[...]
-    copy_f.wait()
-    grads_ref[...] = rg[...]
-
-
-def build(mesh, dims, interpret=False):
+    for k in range(chunks):
+        over[k].wait()
+        grads_ref[:, k] = rg[:, k]
+
+
+def finish(gx_ref, grads_ref, gxt_ref, gin_ref, gout_ref):
+    @pl.when(pl.program_id(0) == 0)
+    def _():
+        rows = gx_ref.shape[0] * gx_ref.shape[1]
+        gxt_ref[...] = gx_ref[...].reshape(rows, gx_ref.shape[2]).T
+
+    span = gout_ref.shape[1]
+    for h in range(2):
+        gin_ref[:, h * span : (h + 1) * span] = grads_ref[0, 0, :, h].astype(F32).reshape(gin_ref.shape[0], span)
+    gout_ref[...] = grads_ref[1, 0].astype(F32).reshape(gout_ref.shape)
+
+
+def build(mesh, dims):
     ny, nz, nx, nc = dims
     nq, ns, npl = ny * nz, nx * nc, ny * nx
     rows, pairs = nq * ns, nq * ns // 2
@@ -315,11 +343,18 @@
 
     def step(saved_input, cotangent, w_in, bias_in, w_out, residual_logit, branch_scale):
         width, units = saved_input.shape[1], w_in.shape[1]
-        piece = units // npl
         span = 2 * width
+        chunks = span // (npl * 8)
         vmem = pltpu.VMEM
         dma = pltpu.SemaphoreType.DMA
         scratch = [
+            vmem((2, width, rows), BF16),
+            vmem((span, units), BF16),
+            vmem((units,), F32),
+            vmem((units, span), BF16),
+            vmem((span,), F32),
+            vmem((span,), F32),
+            vmem((2, nq, ns, width), BF16),
             vmem((2, nq, ns, width), BF16),
             vmem((2, ns, nq, width), BF16),
             vmem((2, ns, nq, width), BF16),
@@ -337,23 +372,24 @@
             vmem((levels * pairs, units), BF16),
             vmem((levels * pairs, units), BF16),
             vmem((levels * pairs, span), BF16),
-            vmem((2, npl, piece, span), BF16),
-            vmem((npl, piece, span), BF16),
-            vmem((npl, piece, span), BF16),
-            vmem((npl, piece, span), BF16),
-            vmem((nz, piece, span), BF16),
-            vmem((2, npl, piece, span), BF16),
+            vmem((2, chunks, npl, 2, 8, span), BF16),
+            vmem((chunks, npl, 2, 8, span), BF16),
+            vmem((chunks, npl, 2, 8, span), BF16),
+            vmem((chunks, npl, 2, 8, span), BF16),
+            vmem((chunks, nz, 2, 8, span), BF16),
+            vmem((2, chunks, npl, 2, 8, span), BF16),
             vmem((ns, nq, width), BF16),
             vmem((ns, nq, width), BF16),
             vmem((nq, ns, width), BF16),
             vmem((nq, ns, width), BF16),
+            dma((7,)),
             dma((2, nq - 1)), dma((2, nq - 1)),
             dma((2, ns - 1)), dma((2, ns - 1)),
-            dma, dma,
-            dma((npl - 1,)), dma((npl - 1,)),
-            dma((nz - 1,)), dma((nz - 1,)),
-            dma((npl - 1,)), dma((npl - 1,)),
-            dma, dma,
+            dma((chunks,)), dma((chunks,)),
+            dma((chunks, npl - 1)), dma((chunks, npl - 1)),
+            dma((chunks, nz - 1)), dma((chunks, nz - 1)),
+            dma((chunks, npl - 1)), dma((chunks, npl - 1)),
+            dma((chunks,)), dma((chunks,)),
             dma((ns - 1,)), dma((ns - 1,)),
             dma((nq - 1,)), dma((nq - 1,)),
         ]
@@ -362,20 +398,32 @@
             functools.partial(kernel, dims, float(rows * rows) ** (-0.5)),
             out_shape=(
                 jax.ShapeDtypeStruct((nq, ns, width), BF16),
-                jax.ShapeDtypeStruct((2, npl, piece, span), BF16),
+                jax.ShapeDtypeStruct((2, chunks, npl, 2, 8, span), BF16),
             ),
-            in_specs=[in_vmem] * 7,
+            in_specs=[pl.BlockSpec(memory_space=pl.ANY)] * 7,
             out_specs=(in_vmem, in_vmem),
             scratch_shapes=scratch,
             compiler_params=pltpu.CompilerParams(collective_id=0, has_side_effects=True, vmem_limit_bytes=60 * 2**20),
-        )(
-            saved_input.reshape(nq, ns, width), cotangent.reshape(nq, ns, width), w_in, bias_in.reshape(1, units),
-            w_out, residual_logit.reshape(1, span), branch_scale.reshape(1, span),
-        )
-        parts = grads.reshape(2, units // span, span, span).astype(F32)
-        grad_in = parts[0].transpose(1, 0, 2).reshape(span, units)
-        grad_out = parts[1].reshape(units, span)
-        return gx.reshape(rows, width), grad_in, grad_out
+        )(saved_input.T, cotangent.T, w_in, bias_in, w_out, residual_logit, branch_scale)
+        gxt, grad_in, grad_out = pl.pallas_call(
+            finish,
+            grid=(chunks,),
+            out_shape=(
+                jax.ShapeDtypeStruct((width, rows), BF16),
+                jax.ShapeDtypeStruct((span, units), F32),
+                jax.ShapeDtypeStruct((units, span), F32),
+            ),
+            in_specs=[
+                pl.BlockSpec((nq, ns, width), lambda k: (0, 0, 0)),
+                pl.BlockSpec((2, 1, npl, 2, 8, span), lambda k: (0, k, 0, 0, 0, 0)),
+            ],
+            out_specs=(
+                pl.BlockSpec((width, rows), lambda k: (0, 0)),
+                pl.BlockSpec((span // chunks, units), lambda k: (k, 0)),
+                pl.BlockSpec((units // chunks, span), lambda k: (k, 0)),
+            ),
+        )(gx, grads)
+        return gxt.T, grad_in, grad_out
 
     in_specs = (P("seq", None), P("seq", None), P(), P(), P(), P(), P())
     out_specs = (P("seq", None), P(), P())

time: 85.2 us -> 69.9 us (0.82)
  local copies, waits for them, and re-layouts: 12.3 us -> 0 us
  Pallas kernels: 72.1 us -> 69.1 us
    pallas_call x1, Pallas kernels: 72.1 us -> 65.7 us  [step(): pl.pallas_call(functools.partial(kernel, dims, float(rows * rows) ** (-0....]
    unnamed x3 -> x0, local copies, waits for them, and re-layouts: 4.95 us -> none
    reshape x4 -> x0, local copies, waits for them, and re-layouts: 4.9 us -> none  [the longest x1 1.28 us: step(): branch_scale.reshape(1, span)]
    pallas_call x0 -> x1, Pallas kernels: none -> 3.43 us  [step(): pl.pallas_call(finish, grid=(chunks,), out_shape=(jax.ShapeDtypeStruct((w...]
    slice x1 -> x0, local copies, waits for them, and re-layouts: 2.41 us -> none  [step(): grad_out = parts[1].reshape(units, span)]
where the time goes in v1:
time: 69.9 us; the launch traced here: 69.8 us
  Pallas kernels  69.1 us (99%)
    pallas_call x1, Pallas kernels, step(): pl.pallas_call(functools.partial(kernel, dims, float(rows * rows) ** (-0....  65.7 us
    pallas_call x1, Pallas kernels, step(): pl.pallas_call(finish, grid=(chunks,), out_shape=(jax.ShapeDtypeStruct((w...  3.43 us

profile of v1, /device:TPU:1, one launch (start us, length us, event | category | flops | bytes accessed | tf_op | source)
XLA Modules:
  0.0 69.8 jit_solution(14947182529714652917)
XLA Ops:
  0.6 65.7 %shard_map.94 = (bf16[32,8,192]{2,1,0:T(8,128)(2,1)}, bf16[2,3,16,2,8,384]{5,4,3,2,1,0:T(8,128)(2,1)}) custom-call(bf16[192,256]{1,0:T(8,128)(2,1)} %bitcast.3, bf16[192,256]{1,0:T(8,128)(2,1)} %bitcast.4, bf16[384,768]{1,0:T(8,128)(2,1)} %win_hbm.1, f32[768]{0:T(1024)} %bias_hbm.1, bf16[768,384]{1,0:T(8,128)(2,1)} %wout_hbm.1, f32[384]{0:T(512)} %logit_hbm.1, ...), custom_call_target="tpu_custom_call" | custom-call | tf_op jit(solution)/shard_map/pallas_call | solution.py:397
  66.3 3.4 %shard_map.95 = (bf16[192,256]{1,0:T(8,128)(2,1)}, f32[384,768]{1,0:T(8,128)}, f32[768,384]{1,0:T(8,128)}) custom-call(bf16[32,8,192]{2,1,0:T(8,128)(2,1)} %get-tuple-element.8.gx_ref, bf16[2,3,16,2,8,384]{5,4,3,2,1,0:T(8,128)(2,1)} %get-tuple-element.9.grads_ref), custom_call_target="tpu_custom_call" | custom-call | tf_op jit(solution)/shard_map/pallas_call | solution.py:408

commit v2 on v1

--- a/solution.py
+++ b/solution.py
@@ -56,13 +56,13 @@
 def kernel(
     dims, scale_out,
     xt_hbm, ct_hbm, win_hbm, bias_hbm, wout_hbm, logit_hbm, scale_hbm,
-    gx_ref, grads_ref,
+    gx_out, grads_out,
     xt, win, bias_row, wout, logit_row, scale_row, xs,
     ra, tb, rb, flat, wi, wit, wo, wot, gate, scale,
     nrm, inv, slope, nlc, act, pg, bgc,
     gb, rc, hsum, rd, rz, rg, tx, rx1, tx2, rx2,
     load_sem, a_send, a_recv, b_send, b_recv, c_send, c_recv, d_send, d_recv, z_send, z_recv,
-    e_send, e_recv, f_send, f_recv, u_send, u_recv, v_send, v_recv,
+    e_send, e_recv, f_send, f_recv, u_send, u_recv, v_send, v_recv, out_sem,
 ):
     ny, nz, nx, nc = dims
     nq, ns, npl = ny * nz, nx * nc, ny * nx
@@ -71,15 +71,15 @@
     low_levels = ns.bit_length() - 1
     levels = rows.bit_length() - 1
     me = lax.axis_index("seq")
-    q, s = me // ns, me % ns
-    y, z, xc, c = q // nz, q % nz, s // nc, s % nc
+    q, s = lax.div(me, ns), lax.rem(me, ns)
+    y, z, xc, c = lax.div(q, nz), lax.rem(q, nz), lax.div(s, nc), lax.rem(s, nc)
     plane = y * nx + xc
 
     def id_qs(qq, ss):
         return qq * ns + ss
 
     def id_plane(pp):
-        return (((pp // nx) * nz + z) * nx + pp % nx) * nc + c
+        return ((lax.div(pp, nx) * nz + z) * nx + lax.rem(pp, nx)) * nc + c
 
     def id_z(zz):
         return ((y * nz + zz) * nx + xc) * nc + c
@@ -93,15 +93,15 @@
 
     @pl.loop(1, nq)
     def _(j):
-        greet(id_qs((q + j) % nq, s))
+        greet(id_qs(lax.rem(q + j, nq), s))
 
     @pl.loop(1, ns)
     def _(j):
-        greet(id_qs(q, (s + j) % ns))
+        greet(id_qs(q, lax.rem(s + j, ns)))
 
     for jy in range(1, ny):
         for jx in range(1, nx):
-            greet(id_plane(((y + jy) % ny) * nx + (xc + jx) % nx))
+            greet(((lax.rem(y + jy, ny) * nz + z) * nx + lax.rem(xc + jx, nx)) * nc + c)
 
     operands = (
         (xt_hbm, xt.at[0]), (ct_hbm, xt.at[1]), (logit_hbm, logit_row), (scale_hbm, scale_row), (bias_hbm, bias_row),
@@ -138,35 +138,32 @@
             device_id=(device,), device_id_type=pl.DeviceIdType.MESH,
         )
 
-    def each(count, copy):
+    def bytes_of(ref, sem):
+        return pltpu.make_async_copy(ref, ref, sem)
+
+    def each(count, copy, landing, recv_sem):
         def start():
             @pl.loop(1, count)
             def _(j):
                 copy(j).start()
 
-        def wait():
-            @pl.loop(1, count)
-            def _(j):
-                copy(j).wait()
-
-        return start, wait
+        return start, bytes_of(landing.at[pl.ds(0, count - 1)], recv_sem).wait
 
     def exchange(count, place, src, dst, send_sem, recv_sem, device_of):
         def copy(j):
-            to = (place + j) % count
-            return send(src.at[to], dst.at[place], send_sem.at[j - 1], recv_sem.at[j - 1], device_of(to))
-
-        return each(count, copy)
+            to = lax.rem(place + j, count)
+            return send(src.at[to], dst.at[place], send_sem, recv_sem, device_of(to))
+
+        return each(count, copy, dst, recv_sem)
 
     def spread(count, place, ref, send_sem, recv_sem, device_of):
         def copy(j):
-            to = (place + j) % count
-            return send(ref.at[place], ref.at[place], send_sem.at[j - 1], recv_sem.at[j - 1], device_of(to))
-
-        return each(count, copy)
+            return send(ref.at[place], ref.at[place], send_sem, recv_sem, device_of(lax.rem(place + j, count)))
+
+        return each(count, copy, ref, recv_sem)
 
     def start_a(k):
-        start, wait = exchange(nq, q, xs.at[k], ra.at[k], a_send.at[k], a_recv.at[k], lambda i: id_qs(i, s))
+        start, wait = exchange(nq, q, xs.at[k], ra.at[k], a_send, a_recv.at[k], lambda i: id_qs(i, s))
         start()
         ra[k, q] = xs[k, q]
         return wait
@@ -183,7 +180,7 @@
         put_rows(ra[k])
         for r in range(ns):
             tb[k, r] = strided(r, nq, ns)[:, :width].astype(BF16)
-        start, wait = exchange(ns, s, tb.at[k], rb.at[k], b_send.at[k], b_recv.at[k], lambda i: id_qs(q, i))
+        start, wait = exchange(ns, s, tb.at[k], rb.at[k], b_send, b_recv.at[k], lambda i: id_qs(q, i))
         start()
         rb[k, s] = tb[k, s]
         return wait
@@ -235,6 +232,27 @@
             result = gate[0:1] * paired + scale[0:1] * row_dot(activated, wo[...])
             state = unite(result[:, :PAD], result[:, PAD:], block_of(level))
 
+    chunks = gb.shape[0]
+    half_chunks = chunks // 2
+    span = 2 * width
+    units = act.shape[1]
+    in_rows, out_rows = span // half_chunks, units // half_chunks
+    to_sibling = []
+
+    def start_c(k):
+        to_sibling.append(send(gb.at[k, 1 - c], rc.at[k], c_send, c_recv.at[k], sibling))
+        to_sibling[k].start()
+
+    plane_waits = []
+
+    def start_d(k):
+        to_sibling[k].wait_recv()
+        hsum[k] = (gb[k, c].astype(F32) + rc[k].astype(F32)).astype(BF16)
+        start, wait = exchange(npl, plane, hsum.at[k], rd.at[k], d_send, d_recv.at[k], id_plane)
+        start()
+        plane_waits.append(wait)
+        rd[k, plane] = hsum[k, plane]
+
     wait_b1()
     state = swap_order(load_state(1), ns, nq)
     for level in reversed(range(levels)):
@@ -245,8 +263,21 @@
         branch = scale[0:1] * upstream
         here = pl.ds(level * pairs, pairs)
         bgc[here, :] = narrow(branch[:, :PAD], branch[:, PAD:], width).astype(BF16)
+        if level == 0:
+            for k in range(half_chunks):
+                grad_out = column_dot(act[:, k * out_rows : (k + 1) * out_rows], bgc[...])
+                gb[k] = grad_out.reshape(2, npl, 8, span).astype(BF16)
+                start_c(k)
         preact_grad = (row_dot(branch.astype(BF16), wot[...]) * slope[level]).astype(BF16)
         pg[here, :] = preact_grad
+        if level == 0:
+            for k in range(half_chunks):
+                start_d(k)
+            for k in range(half_chunks):
+                grad_in = column_dot(nlc[:, k * in_rows : (k + 1) * in_rows], pg[...])
+                for h in range(2):
+                    gb[half_chunks + k, h] = grad_in[:, h * span : (h + 1) * span].reshape(npl, 8, span).astype(BF16)
+                start_c(half_chunks + k)
         normed_grad = row_dot(preact_grad, wit[...])
         normed = nrm[level]
         mean_grad = jnp.sum(normed_grad, axis=1, keepdims=True) * (1.0 / (2 * width))
@@ -259,28 +290,22 @@
     start_u()
     rx1[s] = tx[s]
 
-    chunks = gb.shape[1]
-    span = 2 * width
-    units = act.shape[1]
-    in_rows, out_rows = span // chunks, units // chunks
-    to_sibling = []
+    for k in range(half_chunks, chunks):
+        start_d(k)
+
+    def added(ref, count):
+        total = ref[0].astype(F32)
+        for i in range(1, count):
+            total = total + ref[i].astype(F32)
+        return total
+
+    z_waits = []
     for k in range(chunks):
-        grad_in = column_dot(nlc[:, k * in_rows : (k + 1) * in_rows], pg[...])
-        for h in range(2):
-            gb[0, k, :, h] = grad_in[:, h * span : (h + 1) * span].reshape(npl, 8, span).astype(BF16)
-        grad_out = column_dot(act[:, k * out_rows : (k + 1) * out_rows], bgc[...])
-        gb[1, k] = grad_out.reshape(npl, 2, 8, span).astype(BF16)
-        to_sibling.append(send(gb.at[1 - c, k], rc.at[k], c_send.at[k], c_recv.at[k], sibling))
-        to_sibling[k].start()
-
-    plane_waits = []
-    for k in range(chunks):
-        to_sibling[k].wait()
-        hsum[k] = (gb[c, k].astype(F32) + rc[k].astype(F32)).astype(BF16)
-        start, wait = exchange(npl, plane, hsum.at[k], rd.at[k], d_send.at[k], d_recv.at[k], id_plane)
+        plane_waits[k]()
+        rz[k, z] = added(rd.at[k], npl).astype(BF16)
+        start, wait = spread(nz, z, rz.at[k], z_send, z_recv.at[k], id_z)
         start()
-        plane_waits.append(wait)
-        rd[k, plane] = hsum[k, plane]
+        z_waits.append(wait)
 
     wait_u()
     put_rows(rx1[...])
@@ -290,40 +315,43 @@
     start_v()
     rx2[q] = tx2[q]
 
-    def added(ref, count):
-        total = ref[0].astype(F32)
-        for i in range(1, count):
-            total = total + ref[i].astype(F32)
-        return total
-
-    z_waits = []
-    for k in range(chunks):
-        plane_waits[k]()
-        rz[k, z] = added(rd.at[k], npl).astype(BF16)
-        start, wait = spread(nz, z, rz.at[k], z_send.at[k], z_recv.at[k], id_z)
-        start()
-        z_waits.append(wait)
-
     gather_waits = []
     for k in range(chunks):
         z_waits[k]()
-        rg[c, k, plane] = (added(rz.at[k], nz) * scale_out).astype(BF16)
-        start, wait = spread(npl, plane, rg.at[c, k], e_send.at[k], e_recv.at[k], id_plane)
+        rg[k, c, plane] = (added(rz.at[k], nz) * scale_out).astype(BF16)
+        start, wait = spread(npl, plane, rg.at[k, c], e_send, e_recv.at[k], id_plane)
         start()
         gather_waits.append(wait)
     over = []
+
+    def put_result(src, dst):
+        pltpu.make_async_copy(src, dst, out_sem).start()
+
     for k in range(chunks):
         gather_waits[k]()
-        over.append(send(rg.at[c, k], rg.at[c, k], f_send.at[k], f_recv.at[k], sibling))
+        over.append(send(rg.at[k, c], rg.at[k, c], f_send, f_recv.at[k], sibling))
         over[k].start()
+        put_result(rg.at[k, c], grads_out.at[k, c])
     wait_v()
-    gx_ref[...] = rx2[...]
+    put_result(rx2, gx_out)
     for k in range(chunks):
-        over[k].wait()
-        grads_ref[:, k] = rg[:, k]
-
-
-def finish(gx_ref, grads_ref, gxt_ref, gin_ref, gout_ref):
+        over[k].wait_recv()
+        put_result(rg.at[k, 1 - c], grads_out.at[k, 1 - c])
+
+    bytes_of(xs.at[:, pl.ds(0, nq - 1)], a_send).wait()
+    bytes_of(tb.at[:, pl.ds(0, ns - 1)], b_send).wait()
+    bytes_of(rc, c_send).wait()
+    bytes_of(hsum.at[:, pl.ds(0, npl - 1)], d_send).wait()
+    bytes_of(rz.at[:, pl.ds(0, nz - 1)], z_send).wait()
+    bytes_of(hsum.at[:, pl.ds(0, npl - 1)], e_send).wait()
+    bytes_of(rc, f_send).wait()
+    bytes_of(tx.at[pl.ds(0, ns - 1)], u_send).wait()
+    bytes_of(tx2.at[pl.ds(0, nq - 1)], v_send).wait()
+    pltpu.make_async_copy(rx2, gx_out, out_sem).wait()
+    pltpu.make_async_copy(rg, grads_out, out_sem).wait()
+
+
+def finish(gx_ref, out_ref, in_ref, gxt_ref, gin_ref, gout_ref):
     @pl.when(pl.program_id(0) == 0)
     def _():
         rows = gx_ref.shape[0] * gx_ref.shape[1]
@@ -331,8 +359,8 @@
 
     span = gout_ref.shape[1]
     for h in range(2):
-        gin_ref[:, h * span : (h + 1) * span] = grads_ref[0, 0, :, h].astype(F32).reshape(gin_ref.shape[0], span)
-    gout_ref[...] = grads_ref[1, 0].astype(F32).reshape(gout_ref.shape)
+        gin_ref[:, h * span : (h + 1) * span] = in_ref[0, h].astype(F32).reshape(gin_ref.shape[0], span)
+    gout_ref[...] = out_ref[0].astype(F32).reshape(gout_ref.shape)
 
 
 def build(mesh, dims):
@@ -344,7 +372,8 @@
     def step(saved_input, cotangent, w_in, bias_in, w_out, residual_logit, branch_scale):
         width, units = saved_input.shape[1], w_in.shape[1]
         span = 2 * width
-        chunks = span // (npl * 8)
+        half_chunks = span // (npl * 8)
+        chunks = 2 * half_chunks
         vmem = pltpu.VMEM
         dma = pltpu.SemaphoreType.DMA
         scratch = [
@@ -372,42 +401,42 @@
             vmem((levels * pairs, units), BF16),
             vmem((levels * pairs, units), BF16),
             vmem((levels * pairs, span), BF16),
-            vmem((2, chunks, npl, 2, 8, span), BF16),
-            vmem((chunks, npl, 2, 8, span), BF16),
-            vmem((chunks, npl, 2, 8, span), BF16),
-            vmem((chunks, npl, 2, 8, span), BF16),
-            vmem((chunks, nz, 2, 8, span), BF16),
-            vmem((2, chunks, npl, 2, 8, span), BF16),
+            vmem((chunks, 2, npl, 8, span), BF16),
+            vmem((chunks, npl, 8, span), BF16),
+            vmem((chunks, npl, 8, span), BF16),
+            vmem((chunks, npl, 8, span), BF16),
+            vmem((chunks, nz, 8, span), BF16),
+            vmem((chunks, 2, npl, 8, span), BF16),
             vmem((ns, nq, width), BF16),
             vmem((ns, nq, width), BF16),
             vmem((nq, ns, width), BF16),
             vmem((nq, ns, width), BF16),
             dma((7,)),
-            dma((2, nq - 1)), dma((2, nq - 1)),
-            dma((2, ns - 1)), dma((2, ns - 1)),
-            dma((chunks,)), dma((chunks,)),
-            dma((chunks, npl - 1)), dma((chunks, npl - 1)),
-            dma((chunks, nz - 1)), dma((chunks, nz - 1)),
-            dma((chunks, npl - 1)), dma((chunks, npl - 1)),
-            dma((chunks,)), dma((chunks,)),
-            dma((ns - 1,)), dma((ns - 1,)),
-            dma((nq - 1,)), dma((nq - 1,)),
+            dma, dma((2,)),
+            dma, dma((2,)),
+            dma, dma((chunks,)),
+            dma, dma((chunks,)),
+            dma, dma((chunks,)),
+            dma, dma((chunks,)),
+            dma, dma((chunks,)),
+            dma, dma,
+            dma, dma,
+            dma,
         ]
-        in_vmem = pl.BlockSpec(memory_space=pltpu.VMEM)
         gx, grads = pl.pallas_call(
             functools.partial(kernel, dims, float(rows * rows) ** (-0.5)),
             out_shape=(
                 jax.ShapeDtypeStruct((nq, ns, width), BF16),
-                jax.ShapeDtypeStruct((2, chunks, npl, 2, 8, span), BF16),
+                jax.ShapeDtypeStruct((chunks, 2, npl, 8, span), BF16),
             ),
             in_specs=[pl.BlockSpec(memory_space=pl.ANY)] * 7,
-            out_specs=(in_vmem, in_vmem),
+            out_specs=(pl.BlockSpec(memory_space=pl.ANY),) * 2,
             scratch_shapes=scratch,
-            compiler_params=pltpu.CompilerParams(collective_id=0, has_side_effects=True, vmem_limit_bytes=60 * 2**20),
+            compiler_params=pltpu.CompilerParams(collective_id=0, has_side_effects=True, vmem_limit_bytes=62 * 2**20),
         )(saved_input.T, cotangent.T, w_in, bias_in, w_out, residual_logit, branch_scale)
         gxt, grad_in, grad_out = pl.pallas_call(
             finish,
-            grid=(chunks,),
+            grid=(half_chunks,),
             out_shape=(
                 jax.ShapeDtypeStruct((width, rows), BF16),
                 jax.ShapeDtypeStruct((span, units), F32),
@@ -415,14 +444,15 @@
             ),
             in_specs=[
                 pl.BlockSpec((nq, ns, width), lambda k: (0, 0, 0)),
-                pl.BlockSpec((2, 1, npl, 2, 8, span), lambda k: (0, k, 0, 0, 0, 0)),
+                pl.BlockSpec((1, 2, npl, 8, span), lambda k: (k, 0, 0, 0, 0)),
+                pl.BlockSpec((1, 2, npl, 8, span), lambda k: (half_chunks + k, 0, 0, 0, 0)),
             ],
             out_specs=(
                 pl.BlockSpec((width, rows), lambda k: (0, 0)),
-                pl.BlockSpec((span // chunks, units), lambda k: (k, 0)),
-                pl.BlockSpec((units // chunks, span), lambda k: (k, 0)),
+                pl.BlockSpec((span // half_chunks, units), lambda k: (k, 0)),
+                pl.BlockSpec((units // half_chunks, span), lambda k: (k, 0)),
             ),
-        )(gx, grads)
+        )(gx, grads, grads)
         return gxt.T, grad_in, grad_out
 
     in_specs = (P("seq", None), P("seq", None), P(), P(), P(), P(), P())

time: 69.9 us -> 64.7 us (0.926)
  Pallas kernels: 69.1 us -> 63.9 us
    pallas_call x1, Pallas kernels: 65.7 us -> 60.2 us  [step(): pl.pallas_call(functools.partial(kernel, dims, float(rows * rows) ** (-0....]
where the time goes in v2:
time: 64.7 us; the launch traced here: 64.6 us
  Pallas kernels  63.9 us (99%)
    pallas_call x1, Pallas kernels, step(): pl.pallas_call(functools.partial(kernel, dims, float(rows * rows) ** (-0....  60.2 us
    pallas_call x1, Pallas kernels, step(): pl.pallas_call(finish, grid=(half_chunks,), out_shape=(jax.ShapeDtypeStru...  3.7 us

profile of v2, /device:TPU:1, one launch (start us, length us, event | category | flops | bytes accessed | tf_op | source)
XLA Modules:
  0.0 64.6 jit_solution(13618949491121086807)
XLA Ops:
  0.6 60.2 %shard_map.94 = (bf16[32,8,192]{2,1,0:T(8,128)(2,1)}, bf16[6,2,16,8,384]{4,3,2,1,0:T(8,128)(2,1)}) custom-call(bf16[192,256]{1,0:T(8,128)(2,1)} %bitcast.3, bf16[192,256]{1,0:T(8,128)(2,1)} %bitcast.4, bf16[384,768]{1,0:T(8,128)(2,1)} %win_hbm.1, f32[768]{0:T(1024)} %bias_hbm.1, bf16[768,384]{1,0:T(8,128)(2,1)} %wout_hbm.1, f32[384]{0:T(512)} %logit_hbm.1, ...), custom_call_target="tpu_custom_call" | custom-call | tf_op jit(solution)/shard_map/pallas_call | solution.py:426
  60.9 3.7 %shard_map.95 = (bf16[192,256]{1,0:T(8,128)(2,1)}, f32[384,768]{1,0:T(8,128)}, f32[768,384]{1,0:T(8,128)}) custom-call(bf16[32,8,192]{2,1,0:T(8,128)(2,1)} %get-tuple-element.8.gx_ref, bf16[6,2,16,8,384]{4,3,2,1,0:T(8,128)(2,1)} %get-tuple-element.9.out_ref.in_ref, bf16[6,2,16,8,384]{4,3,2,1,0:T(8,128)(2,1)} %get-tuple-element.9.out_ref.in_ref), custom_call_target="tpu_custom_call" | custom-call | tf_op jit(solution)/shard_map/pallas_call | solution.py:437

commit v3 on v2

--- a/solution.py
+++ b/solution.py
@@ -65,43 +65,45 @@
     e_send, e_recv, f_send, f_recv, u_send, u_recv, v_send, v_recv, out_sem,
 ):
     ny, nz, nx, nc = dims
-    nq, ns, npl = ny * nz, nx * nc, ny * nx
-    rows, pairs = nq * ns, nq * ns // 2
+    ns, npl = nx * nc, ny * nx
+    ng = ny * ns
+    rows, pairs = nz * ng, nz * ng // 2
     width = xt.shape[1]
-    low_levels = ns.bit_length() - 1
+    low_levels, mid_levels = ns.bit_length() - 1, (ns * nz).bit_length() - 1
     levels = rows.bit_length() - 1
     me = lax.axis_index("seq")
     q, s = lax.div(me, ns), lax.rem(me, ns)
     y, z, xc, c = lax.div(q, nz), lax.rem(q, nz), lax.div(s, nc), lax.rem(s, nc)
     plane = y * nx + xc
 
-    def id_qs(qq, ss):
-        return qq * ns + ss
+    group = y * ns + s
+
+    def id_of(zz, gg):
+        return (lax.div(gg, ns) * nz + zz) * ns + lax.rem(gg, ns)
 
     def id_plane(pp):
         return ((lax.div(pp, nx) * nz + z) * nx + lax.rem(pp, nx)) * nc + c
 
     def id_z(zz):
-        return ((y * nz + zz) * nx + xc) * nc + c
-
-    sibling = id_qs(q, xc * nc + (1 - c))
+        return id_of(zz, group)
+
+    def id_group(gg):
+        return id_of(z, gg)
+
+    sibling = id_group(group + 1 - 2 * c)
 
     barrier = pltpu.get_barrier_semaphore()
 
     def greet(device):
         pl.semaphore_signal(barrier, inc=1, device_id=(device,), device_id_type=pl.DeviceIdType.MESH)
 
-    @pl.loop(1, nq)
+    @pl.loop(1, nz)
     def _(j):
-        greet(id_qs(lax.rem(q + j, nq), s))
-
-    @pl.loop(1, ns)
+        greet(id_z(lax.rem(z + j, nz)))
+
+    @pl.loop(1, ng)
     def _(j):
-        greet(id_qs(q, lax.rem(s + j, ns)))
-
-    for jy in range(1, ny):
-        for jx in range(1, nx):
-            greet(((lax.rem(y + jy, ny) * nz + z) * nx + lax.rem(xc + jx, nx)) * nc + c)
+        greet(id_group(lax.rem(group + j, ng)))
 
     operands = (
         (xt_hbm, xt.at[0]), (ct_hbm, xt.at[1]), (logit_hbm, logit_row), (scale_hbm, scale_row), (bias_hbm, bias_row),
@@ -113,7 +115,7 @@
     flat[...] = jnp.zeros_like(flat)
     for k in range(2):
         loads[k].wait()
-        xs[k] = xt[k].T.reshape(nq, ns, width)
+        xs[k] = xt[k].T.reshape(nz, ng, width)
     for load in loads[2:]:
         load.wait()
     wide_in = jnp.zeros((PAD - width, win.shape[1]), BF16)
@@ -130,7 +132,7 @@
     lane = lax.broadcasted_iota(jnp.int32, (1, 2 * PAD), 1) % PAD
     mask = jnp.where(lane < width, 1.0, 0.0)
 
-    pl.semaphore_wait(barrier, (nq - 1) + (ns - 1) + (ny - 1) * (nx - 1))
+    pl.semaphore_wait(barrier, (nz - 1) + (ng - 1))
 
     def send(src, dst, send_sem, recv_sem, device):
         return pltpu.make_async_remote_copy(
@@ -163,9 +165,9 @@
         return each(count, copy, ref, recv_sem)
 
     def start_a(k):
-        start, wait = exchange(nq, q, xs.at[k], ra.at[k], a_send, a_recv.at[k], lambda i: id_qs(i, s))
+        start, wait = exchange(nz, z, xs.at[k], ra.at[k], a_send, a_recv.at[k], id_z)
         start()
-        ra[k, q] = xs[k, q]
+        ra[k, z] = xs[k, z]
         return wait
 
     def put_rows(block):
@@ -178,11 +180,11 @@
 
     def start_b(k):
         put_rows(ra[k])
-        for r in range(ns):
-            tb[k, r] = strided(r, nq, ns)[:, :width].astype(BF16)
-        start, wait = exchange(ns, s, tb.at[k], rb.at[k], b_send, b_recv.at[k], lambda i: id_qs(q, i))
+        for g in range(ng):
+            tb[k, g] = strided(g, nz, ng)[:, :width].astype(BF16)
+        start, wait = exchange(ng, group, tb.at[k], rb.at[k], b_send, b_recv.at[k], id_group)
         start()
-        rb[k, s] = tb[k, s]
+        rb[k, group] = tb[k, group]
         return wait
 
     wait_a0 = start_a(0)
@@ -203,12 +205,14 @@
         return jnp.concatenate([strided(j, major, minor) for j in range(minor)], axis=0)
 
     def block_of(level):
-        return nq * 2**level if level < low_levels else 2**level
+        if level < low_levels:
+            return nz * 2**level
+        return ng * 2 ** (level - low_levels) if level < mid_levels else ns * 2 ** (level - mid_levels)
 
     state = load_state(0)
     for level in range(levels):
         if level == low_levels:
-            state = swap_order(state, ns, nq)
+            state = swap_order(state, ng, nz)
         first, second = halves(state, block_of(level))
         paired = jnp.concatenate([first, second], axis=1)
         average = jnp.sum(paired, axis=1, keepdims=True) * (1.0 / (2 * width))
@@ -223,10 +227,11 @@
         square = preact * preact
         tangent = jnp.tanh(preact * (tanh_scale + (tanh_scale * cubic_coef) * square))
         half = 0.5 + 0.5 * tangent
-        activated = (preact * half).astype(BF16)
+        product = preact * half
+        activated = product.astype(BF16)
         act[here, :] = activated
-        slope[level] = half + (0.5 * preact) * (1.0 - tangent * tangent) * (
-            tanh_scale + (3.0 * tanh_scale * cubic_coef) * square
+        slope[level] = half + (product - product * half) * (
+            (2.0 * tanh_scale) + (6.0 * tanh_scale * cubic_coef) * square
         )
         if level + 1 < levels:
             result = gate[0:1] * paired + scale[0:1] * row_dot(activated, wo[...])
@@ -247,37 +252,36 @@
 
     def start_d(k):
         to_sibling[k].wait_recv()
-        hsum[k] = (gb[k, c].astype(F32) + rc[k].astype(F32)).astype(BF16)
+        hsum[k] = gb[k, c] + rc[k]
         start, wait = exchange(npl, plane, hsum.at[k], rd.at[k], d_send, d_recv.at[k], id_plane)
         start()
         plane_waits.append(wait)
         rd[k, plane] = hsum[k, plane]
 
     wait_b1()
-    state = swap_order(load_state(1), ns, nq)
+    state = swap_order(load_state(1), ng, nz)
     for level in reversed(range(levels)):
         if level == low_levels - 1:
-            state = swap_order(state, nq, ns)
+            state = swap_order(state, nz, ng)
         first, second = halves(state, block_of(level))
         upstream = jnp.concatenate([first, second], axis=1)
         branch = scale[0:1] * upstream
         here = pl.ds(level * pairs, pairs)
         bgc[here, :] = narrow(branch[:, :PAD], branch[:, PAD:], width).astype(BF16)
+        preact_grad = (row_dot(branch.astype(BF16), wot[...]) * slope[level]).astype(BF16)
+        pg[here, :] = preact_grad
         if level == 0:
             for k in range(half_chunks):
                 grad_out = column_dot(act[:, k * out_rows : (k + 1) * out_rows], bgc[...])
                 gb[k] = grad_out.reshape(2, npl, 8, span).astype(BF16)
                 start_c(k)
-        preact_grad = (row_dot(branch.astype(BF16), wot[...]) * slope[level]).astype(BF16)
-        pg[here, :] = preact_grad
-        if level == 0:
-            for k in range(half_chunks):
-                start_d(k)
             for k in range(half_chunks):
                 grad_in = column_dot(nlc[:, k * in_rows : (k + 1) * in_rows], pg[...])
                 for h in range(2):
                     gb[half_chunks + k, h] = grad_in[:, h * span : (h + 1) * span].reshape(npl, 8, span).astype(BF16)
                 start_c(half_chunks + k)
+            for k in range(chunks):
+                start_d(k)
         normed_grad = row_dot(preact_grad, wit[...])
         normed = nrm[level]
         mean_grad = jnp.sum(normed_grad, axis=1, keepdims=True) * (1.0 / (2 * width))
@@ -285,13 +289,10 @@
         grad = gate[0:1] * upstream + inv[level] * (normed_grad - mean_grad * mask - normed * mean_both)
         state = unite(grad[:, :PAD], grad[:, PAD:], block_of(level))
 
-    tx[...] = state[:, :width].reshape(ns, nq, width).astype(BF16)
-    start_u, wait_u = exchange(ns, s, tx, rx1, u_send, u_recv, lambda i: id_qs(q, i))
+    tx[...] = state[:, :width].reshape(ng, nz, width).astype(BF16)
+    start_u, wait_u = exchange(ng, group, tx, rx1, u_send, u_recv, id_group)
     start_u()
-    rx1[s] = tx[s]
-
-    for k in range(half_chunks, chunks):
-        start_d(k)
+    rx1[group] = tx[group]
 
     def added(ref, count):
         total = ref[0].astype(F32)
@@ -309,11 +310,11 @@
 
     wait_u()
     put_rows(rx1[...])
-    for j in range(nq):
-        tx2[j] = strided(j, ns, nq)[:, :width].astype(BF16)
-    start_v, wait_v = exchange(nq, q, tx2, rx2, v_send, v_recv, lambda i: id_qs(i, s))
+    for j in range(nz):
+        tx2[j] = strided(j, ng, nz)[:, :width].astype(BF16)
+    start_v, wait_v = exchange(nz, z, tx2, rx2, v_send, v_recv, id_z)
     start_v()
-    rx2[q] = tx2[q]
+    rx2[z] = tx2[z]
 
     gather_waits = []
     for k in range(chunks):
@@ -338,35 +339,52 @@
         over[k].wait_recv()
         put_result(rg.at[k, 1 - c], grads_out.at[k, 1 - c])
 
-    bytes_of(xs.at[:, pl.ds(0, nq - 1)], a_send).wait()
-    bytes_of(tb.at[:, pl.ds(0, ns - 1)], b_send).wait()
+    bytes_of(xs.at[:, pl.ds(0, nz - 1)], a_send).wait()
+    bytes_of(tb.at[:, pl.ds(0, ng - 1)], b_send).wait()
     bytes_of(rc, c_send).wait()
     bytes_of(hsum.at[:, pl.ds(0, npl - 1)], d_send).wait()
     bytes_of(rz.at[:, pl.ds(0, nz - 1)], z_send).wait()
     bytes_of(hsum.at[:, pl.ds(0, npl - 1)], e_send).wait()
     bytes_of(rc, f_send).wait()
-    bytes_of(tx.at[pl.ds(0, ns - 1)], u_send).wait()
-    bytes_of(tx2.at[pl.ds(0, nq - 1)], v_send).wait()
+    bytes_of(tx.at[pl.ds(0, ng - 1)], u_send).wait()
+    bytes_of(tx2.at[pl.ds(0, nz - 1)], v_send).wait()
     pltpu.make_async_copy(rx2, gx_out, out_sem).wait()
     pltpu.make_async_copy(rg, grads_out, out_sem).wait()
 
 
-def finish(gx_ref, out_ref, in_ref, gxt_ref, gin_ref, gout_ref):
-    @pl.when(pl.program_id(0) == 0)
-    def _():
-        rows = gx_ref.shape[0] * gx_ref.shape[1]
-        gxt_ref[...] = gx_ref[...].reshape(rows, gx_ref.shape[2]).T
-
-    span = gout_ref.shape[1]
-    for h in range(2):
-        gin_ref[:, h * span : (h + 1) * span] = in_ref[0, h].astype(F32).reshape(gin_ref.shape[0], span)
-    gout_ref[...] = out_ref[0].astype(F32).reshape(gout_ref.shape)
+def finish(gx_hbm, grads_hbm, gxt_hbm, gin_hbm, gout_hbm, gx, grads, gxt, gin, gout, in_sem, out_sem):
+    chunks = grads.shape[0]
+    half_chunks = chunks // 2
+    span, units = gin.shape
+    in_rows, out_rows = span // half_chunks, units // half_chunks
+    loads = [pltpu.make_async_copy(grads_hbm.at[k], grads.at[k], in_sem.at[k]) for k in range(chunks)]
+    loads.append(pltpu.make_async_copy(gx_hbm, gx, in_sem.at[chunks]))
+    for load in loads:
+        load.start()
+    for k in range(half_chunks):
+        loads[k].wait()
+        here = pl.ds(k * out_rows, out_rows)
+        gout[here, :] = grads[k].astype(F32).reshape(out_rows, span)
+        pltpu.make_async_copy(gout.at[here], gout_hbm.at[here], out_sem.at[0]).start()
+    for k in range(half_chunks):
+        loads[half_chunks + k].wait()
+        here = pl.ds(k * in_rows, in_rows)
+        for h in range(2):
+            gin[here, h * span : (h + 1) * span] = grads[half_chunks + k, h].astype(F32).reshape(in_rows, span)
+        pltpu.make_async_copy(gin.at[here], gin_hbm.at[here], out_sem.at[1]).start()
+    loads[chunks].wait()
+    gxt[...] = gx[...].reshape(gxt.shape[1], gxt.shape[0]).T
+    last = pltpu.make_async_copy(gxt, gxt_hbm, out_sem.at[2])
+    last.start()
+    pltpu.make_async_copy(gout, gout_hbm, out_sem.at[0]).wait()
+    pltpu.make_async_copy(gin, gin_hbm, out_sem.at[1]).wait()
+    last.wait()
 
 
 def build(mesh, dims):
     ny, nz, nx, nc = dims
-    nq, ns, npl = ny * nz, nx * nc, ny * nx
-    rows, pairs = nq * ns, nq * ns // 2
+    npl, ng = ny * nx, ny * nx * nc
+    rows, pairs = nz * ng, nz * ng // 2
     levels = rows.bit_length() - 1
 
     def step(saved_input, cotangent, w_in, bias_in, w_out, residual_logit, branch_scale):
@@ -383,10 +401,10 @@
             vmem((units, span), BF16),
             vmem((span,), F32),
             vmem((span,), F32),
-            vmem((2, nq, ns, width), BF16),
-            vmem((2, nq, ns, width), BF16),
-            vmem((2, ns, nq, width), BF16),
-            vmem((2, ns, nq, width), BF16),
+            vmem((2, nz, ng, width), BF16),
+            vmem((2, nz, ng, width), BF16),
+            vmem((2, ng, nz, width), BF16),
+            vmem((2, ng, nz, width), BF16),
             vmem((2, rows, LANES), F32),
             vmem((2 * PAD, units), BF16),
             vmem((units, 2 * PAD), BF16),
@@ -407,10 +425,10 @@
             vmem((chunks, npl, 8, span), BF16),
             vmem((chunks, nz, 8, span), BF16),
             vmem((chunks, 2, npl, 8, span), BF16),
-            vmem((ns, nq, width), BF16),
-            vmem((ns, nq, width), BF16),
-            vmem((nq, ns, width), BF16),
-            vmem((nq, ns, width), BF16),
+            vmem((ng, nz, width), BF16),
+            vmem((ng, nz, width), BF16),
+            vmem((nz, ng, width), BF16),
+            vmem((nz, ng, width), BF16),
             dma((7,)),
             dma, dma((2,)),
             dma, dma((2,)),
@@ -426,7 +444,7 @@
         gx, grads = pl.pallas_call(
             functools.partial(kernel, dims, float(rows * rows) ** (-0.5)),
             out_shape=(
-                jax.ShapeDtypeStruct((nq, ns, width), BF16),
+                jax.ShapeDtypeStruct((nz, ng, width), BF16),
                 jax.ShapeDtypeStruct((chunks, 2, npl, 8, span), BF16),
             ),
             in_specs=[pl.BlockSpec(memory_space=pl.ANY)] * 7,
@@ -436,23 +454,20 @@
         )(saved_input.T, cotangent.T, w_in, bias_in, w_out, residual_logit, branch_scale)
         gxt, grad_in, grad_out = pl.pallas_call(
             finish,
-            grid=(half_chunks,),
             out_shape=(
                 jax.ShapeDtypeStruct((width, rows), BF16),
                 jax.ShapeDtypeStruct((span, units), F32),
                 jax.ShapeDtypeStruct((units, span), F32),
             ),
-            in_specs=[
-                pl.BlockSpec((nq, ns, width), lambda k: (0, 0, 0)),
-                pl.BlockSpec((1, 2, npl, 8, span), lambda k: (k, 0, 0, 0, 0)),
-                pl.BlockSpec((1, 2, npl, 8, span), lambda k: (half_chunks + k, 0, 0, 0, 0)),
+            in_specs=[pl.BlockSpec(memory_space=pl.ANY)] * 2,
+            out_specs=(pl.BlockSpec(memory_space=pl.ANY),) * 3,
+            scratch_shapes=[
+                vmem(gx.shape, BF16), vmem(grads.shape, BF16),
+                vmem((width, rows), BF16), vmem((span, units), F32), vmem((units, span), F32),
+                dma((chunks + 1,)), dma((3,)),
             ],
-            out_specs=(
-                pl.BlockSpec((width, rows), lambda k: (0, 0)),
-                pl.BlockSpec((span // half_chunks, units), lambda k: (k, 0)),
-                pl.BlockSpec((units // half_chunks, span), lambda k: (k, 0)),
-            ),
-        )(gx, grads, grads)
+            compiler_params=pltpu.CompilerParams(vmem_limit_bytes=62 * 2**20),
+        )(gx, grads)
         return gxt.T, grad_in, grad_out
 
     in_specs = (P("seq", None), P("seq", None), P(), P(), P(), P(), P())

time: 64.7 us -> 62.2 us (0.961)
  Pallas kernels: 63.9 us -> 61.4 us
    pallas_call x1, Pallas kernels: 60.2 us -> 59 us  [step(): pl.pallas_call(functools.partial(kernel, dims, float(rows * rows) ** (-0....]
    pallas_call x1, Pallas kernels: 3.7 us -> 2.46 us  [step(): pl.pallas_call(finish, out_shape=(jax.ShapeDtypeStruct((width, rows), BF1...]
where the time goes in v3:
time: 62.2 us; the launch traced here: 62.1 us
  Pallas kernels  61.4 us (99%)
  between operations  0.64 us (1%)
    pallas_call x1, Pallas kernels, step(): pl.pallas_call(functools.partial(kernel, dims, float(rows * rows) ** (-0....  59 us
    pallas_call x1, Pallas kernels, step(): pl.pallas_call(finish, out_shape=(jax.ShapeDtypeStruct((width, rows), BF1...  2.46 us

profile of v3, /device:TPU:1, one launch (start us, length us, event | category | flops | bytes accessed | tf_op | source)
XLA Modules:
  0.0 62.1 jit_solution(18438139425753605555)
XLA Ops:
  0.6 59.0 %shard_map.94 = (bf16[8,32,192]{2,1,0:T(8,128)(2,1)}, bf16[6,2,16,8,384]{4,3,2,1,0:T(8,128)(2,1)}) custom-call(bf16[192,256]{1,0:T(8,128)(2,1)} %bitcast.3, bf16[192,256]{1,0:T(8,128)(2,1)} %bitcast.4, bf16[384,768]{1,0:T(8,128)(2,1)} %win_hbm.1, f32[768]{0:T(1024)} %bias_hbm.1, bf16[768,384]{1,0:T(8,128)(2,1)} %wout_hbm.1, f32[384]{0:T(512)} %logit_hbm.1, ...), custom_call_target="tpu_custom_call" | custom-call | tf_op jit(solution)/shard_map/pallas_call | solution.py:444
  59.6 2.5 %shard_map.95 = (bf16[192,256]{1,0:T(8,128)(2,1)}, f32[384,768]{1,0:T(8,128)}, f32[768,384]{1,0:T(8,128)}) custom-call(bf16[8,32,192]{2,1,0:T(8,128)(2,1)} %get-tuple-element.8.gx_hbm, bf16[6,2,16,8,384]{4,3,2,1,0:T(8,128)(2,1)} %get-tuple-element.9.grads_hbm), custom_call_target="tpu_custom_call" | custom-call | tf_op jit(solution)/shard_map/pallas_call | solution.py:455

commit v4 on v3

--- a/solution.py
+++ b/solution.py
@@ -113,9 +113,27 @@
     for load in loads:
         load.start()
     flat[...] = jnp.zeros_like(flat)
+    def put_rows(block):
+        values = block.astype(F32).reshape(rows, width)
+        flat[0] = values[:, :LANES]
+        flat[1, :, : width - LANES] = values[:, LANES:]
+
+    def fold():
+        tails = flat[1].reshape(nz, 2, ng // 2, LANES)
+        moved = pltpu.roll(tails[:, 1].reshape(rows // 2, LANES), width - LANES, 1)
+        both = tails[:, 0] + moved.reshape(nz, ng // 2, LANES)
+        return jnp.concatenate([flat[0].reshape(nz, ng, LANES), both], axis=1).astype(BF16)
+
+    def unfold(block):
+        both = block[:, ng:].astype(F32)
+        moved = pltpu.roll(both.reshape(rows // 2, LANES), 2 * LANES - width, 1).reshape(nz, ng // 2, LANES)
+        flat[0] = block[:, :ng].astype(F32).reshape(rows, LANES)
+        flat[1, :, : width - LANES] = jnp.concatenate([both, moved], axis=1).reshape(rows, LANES)[:, : width - LANES]
+
     for k in range(2):
         loads[k].wait()
-        xs[k] = xt[k].T.reshape(nz, ng, width)
+        put_rows(xt[k].T)
+        xs[k] = fold()
     for load in loads[2:]:
         load.wait()
     wide_in = jnp.zeros((PAD - width, win.shape[1]), BF16)
@@ -170,16 +188,11 @@
         ra[k, z] = xs[k, z]
         return wait
 
-    def put_rows(block):
-        values = block.astype(F32).reshape(rows, width)
-        flat[0] = values[:, :LANES]
-        flat[1, :, : width - LANES] = values[:, LANES:]
-
     def strided(start, size, stride):
         return jnp.concatenate([flat[h, pl.ds(start, size, stride=stride), :] for h in range(2)], axis=1)
 
     def start_b(k):
-        put_rows(ra[k])
+        unfold(ra[k])
         for g in range(ng):
             tb[k, g] = strided(g, nz, ng)[:, :width].astype(BF16)
         start, wait = exchange(ng, group, tb.at[k], rb.at[k], b_send, b_recv.at[k], id_group)
@@ -268,20 +281,22 @@
         branch = scale[0:1] * upstream
         here = pl.ds(level * pairs, pairs)
         bgc[here, :] = narrow(branch[:, :PAD], branch[:, PAD:], width).astype(BF16)
+        if level == 0:
+            grad_out = column_dot(act[...], bgc[...])
+            for k in range(half_chunks):
+                gb[k] = grad_out[k * out_rows : (k + 1) * out_rows].reshape(2, npl, 8, span).astype(BF16)
+                start_c(k)
         preact_grad = (row_dot(branch.astype(BF16), wot[...]) * slope[level]).astype(BF16)
         pg[here, :] = preact_grad
         if level == 0:
             for k in range(half_chunks):
-                grad_out = column_dot(act[:, k * out_rows : (k + 1) * out_rows], bgc[...])
-                gb[k] = grad_out.reshape(2, npl, 8, span).astype(BF16)
-                start_c(k)
+                start_d(k)
+            grad_in = column_dot(nlc[...], pg[...])
             for k in range(half_chunks):
-                grad_in = column_dot(nlc[:, k * in_rows : (k + 1) * in_rows], pg[...])
                 for h in range(2):
-                    gb[half_chunks + k, h] = grad_in[:, h * span : (h + 1) * span].reshape(npl, 8, span).astype(BF16)
+                    part = grad_in[k * in_rows : (k + 1) * in_rows, h * span : (h + 1) * span]
+                    gb[half_chunks + k, h] = part.reshape(npl, 8, span).astype(BF16)
                 start_c(half_chunks + k)
-            for k in range(chunks):
-                start_d(k)
         normed_grad = row_dot(preact_grad, wit[...])
         normed = nrm[level]
         mean_grad = jnp.sum(normed_grad, axis=1, keepdims=True) * (1.0 / (2 * width))
@@ -292,6 +307,8 @@
     tx[...] = state[:, :width].reshape(ng, nz, width).astype(BF16)
     start_u, wait_u = exchange(ng, group, tx, rx1, u_send, u_recv, id_group)
     start_u()
+    for k in range(half_chunks, chunks):
+        start_d(k)
     rx1[group] = tx[group]
 
     def added(ref, count):
@@ -308,13 +325,15 @@
         start()
         z_waits.append(wait)
 
-    wait_u()
-    put_rows(rx1[...])
-    for j in range(nz):
-        tx2[j] = strided(j, ng, nz)[:, :width].astype(BF16)
-    start_v, wait_v = exchange(nz, z, tx2, rx2, v_send, v_recv, id_z)
-    start_v()
-    rx2[z] = tx2[z]
+    def return_rows():
+        wait_u()
+        put_rows(rx1[...])
+        for j in range(nz):
+            tx2[j] = strided(j, ng, nz)[:, :width].astype(BF16)
+        start_v, wait_v = exchange(nz, z, tx2, rx2, v_send, v_recv, id_z)
+        start_v()
+        rx2[z] = tx2[z]
+        return wait_v
 
     gather_waits = []
     for k in range(chunks):
@@ -323,6 +342,8 @@
         start, wait = spread(npl, plane, rg.at[k, c], e_send, e_recv.at[k], id_plane)
         start()
         gather_waits.append(wait)
+        if k == half_chunks:
+            wait_v = return_rows()
     over = []
 
     def put_result(src, dst):
@@ -401,8 +422,8 @@
             vmem((units, span), BF16),
             vmem((span,), F32),
             vmem((span,), F32),
-            vmem((2, nz, ng, width), BF16),
-            vmem((2, nz, ng, width), BF16),
+            vmem((2, nz, ng + ng // 2, LANES), BF16),
+            vmem((2, nz, ng + ng // 2, LANES), BF16),
             vmem((2, ng, nz, width), BF16),
             vmem((2, ng, nz, width), BF16),
             vmem((2, rows, LANES), F32),

time: 62.2 us -> 60.7 us (0.976)
  Pallas kernels: 61.4 us -> 59.9 us
    pallas_call x1, Pallas kernels: 59 us -> 57.5 us  [step(): pl.pallas_call(functools.partial(kernel, dims, float(rows * rows) ** (-0....]
where the time goes in v4:
time: 60.7 us; the launch traced here: 60.6 us
  Pallas kernels  59.9 us (99%)
  between operations  0.64 us (1%)
    pallas_call x1, Pallas kernels, step(): pl.pallas_call(functools.partial(kernel, dims, float(rows * rows) ** (-0....  57.5 us
    pallas_call x1, Pallas kernels, step(): pl.pallas_call(finish, out_shape=(jax.ShapeDtypeStruct((width, rows), BF1...  2.46 us

profile of v4, /device:TPU:1, one launch (start us, length us, event | category | flops | bytes accessed | tf_op | source)
XLA Modules:
  0.0 60.6 jit_solution(4328174722547897557)
XLA Ops:
  0.6 57.5 %shard_map.94 = (bf16[8,32,192]{2,1,0:T(8,128)(2,1)}, bf16[6,2,16,8,384]{4,3,2,1,0:T(8,128)(2,1)}) custom-call(bf16[192,256]{1,0:T(8,128)(2,1)} %bitcast.3, bf16[192,256]{1,0:T(8,128)(2,1)} %bitcast.4, bf16[384,768]{1,0:T(8,128)(2,1)} %win_hbm.1, f32[768]{0:T(1024)} %bias_hbm.1, bf16[768,384]{1,0:T(8,128)(2,1)} %wout_hbm.1, f32[384]{0:T(512)} %logit_hbm.1, ...), custom_call_target="tpu_custom_call" | custom-call | tf_op jit(solution)/shard_map/pallas_call | solution.py:465
  58.1 2.5 %shard_map.95 = (bf16[192,256]{1,0:T(8,128)(2,1)}, f32[384,768]{1,0:T(8,128)}, f32[768,384]{1,0:T(8,128)}) custom-call(bf16[8,32,192]{2,1,0:T(8,128)(2,1)} %get-tuple-element.8.gx_hbm, bf16[6,2,16,8,384]{4,3,2,1,0:T(8,128)(2,1)} %get-tuple-element.9.grads_hbm), custom_call_target="tpu_custom_call" | custom-call | tf_op jit(solution)/shard_map/pallas_call | solution.py:476

commit v5 on v4

--- a/solution.py
+++ b/solution.py
@@ -56,13 +56,13 @@
 def kernel(
     dims, scale_out,
     xt_hbm, ct_hbm, win_hbm, bias_hbm, wout_hbm, logit_hbm, scale_hbm,
-    gx_out, grads_out,
+    rx2, rg,
     xt, win, bias_row, wout, logit_row, scale_row, xs,
     ra, tb, rb, flat, wi, wit, wo, wot, gate, scale,
     nrm, inv, slope, nlc, act, pg, bgc,
-    gb, rc, hsum, rd, rz, rg, tx, rx1, tx2, rx2,
+    gb, rc, hsum, rd, rz, tx, rx1, tx2,
     load_sem, a_send, a_recv, b_send, b_recv, c_send, c_recv, d_send, d_recv, z_send, z_recv,
-    e_send, e_recv, f_send, f_recv, u_send, u_recv, v_send, v_recv, out_sem,
+    e_send, e_recv, f_send, f_recv, u_send, u_recv, v_send, v_recv,
 ):
     ny, nz, nx, nc = dims
     ns, npl = nx * nc, ny * nx
@@ -306,9 +306,9 @@
 
     tx[...] = state[:, :width].reshape(ng, nz, width).astype(BF16)
     start_u, wait_u = exchange(ng, group, tx, rx1, u_send, u_recv, id_group)
-    start_u()
     for k in range(half_chunks, chunks):
         start_d(k)
+    start_u()
     rx1[group] = tx[group]
 
     def added(ref, count):
@@ -342,23 +342,17 @@
         start, wait = spread(npl, plane, rg.at[k, c], e_send, e_recv.at[k], id_plane)
         start()
         gather_waits.append(wait)
-        if k == half_chunks:
+        if k == chunks - 2:
             wait_v = return_rows()
     over = []
-
-    def put_result(src, dst):
-        pltpu.make_async_copy(src, dst, out_sem).start()
 
     for k in range(chunks):
         gather_waits[k]()
         over.append(send(rg.at[k, c], rg.at[k, c], f_send, f_recv.at[k], sibling))
         over[k].start()
-        put_result(rg.at[k, c], grads_out.at[k, c])
     wait_v()
-    put_result(rx2, gx_out)
     for k in range(chunks):
         over[k].wait_recv()
-        put_result(rg.at[k, 1 - c], grads_out.at[k, 1 - c])
 
     bytes_of(xs.at[:, pl.ds(0, nz - 1)], a_send).wait()
     bytes_of(tb.at[:, pl.ds(0, ng - 1)], b_send).wait()
@@ -369,31 +363,21 @@
     bytes_of(rc, f_send).wait()
     bytes_of(tx.at[pl.ds(0, ng - 1)], u_send).wait()
     bytes_of(tx2.at[pl.ds(0, nz - 1)], v_send).wait()
-    pltpu.make_async_copy(rx2, gx_out, out_sem).wait()
-    pltpu.make_async_copy(rg, grads_out, out_sem).wait()
-
-
-def finish(gx_hbm, grads_hbm, gxt_hbm, gin_hbm, gout_hbm, gx, grads, gxt, gin, gout, in_sem, out_sem):
-    chunks = grads.shape[0]
-    half_chunks = chunks // 2
+
+
+def finish(gx, grads, gxt_hbm, gin_hbm, gout_hbm, gxt, gin, gout, out_sem):
+    half_chunks = grads.shape[0] // 2
     span, units = gin.shape
     in_rows, out_rows = span // half_chunks, units // half_chunks
-    loads = [pltpu.make_async_copy(grads_hbm.at[k], grads.at[k], in_sem.at[k]) for k in range(chunks)]
-    loads.append(pltpu.make_async_copy(gx_hbm, gx, in_sem.at[chunks]))
-    for load in loads:
-        load.start()
     for k in range(half_chunks):
-        loads[k].wait()
         here = pl.ds(k * out_rows, out_rows)
         gout[here, :] = grads[k].astype(F32).reshape(out_rows, span)
         pltpu.make_async_copy(gout.at[here], gout_hbm.at[here], out_sem.at[0]).start()
     for k in range(half_chunks):
-        loads[half_chunks + k].wait()
         here = pl.ds(k * in_rows, in_rows)
         for h in range(2):
             gin[here, h * span : (h + 1) * span] = grads[half_chunks + k, h].astype(F32).reshape(in_rows, span)
         pltpu.make_async_copy(gin.at[here], gin_hbm.at[here], out_sem.at[1]).start()
-    loads[chunks].wait()
     gxt[...] = gx[...].reshape(gxt.shape[1], gxt.shape[0]).T
     last = pltpu.make_async_copy(gxt, gxt_hbm, out_sem.at[2])
     last.start()
@@ -445,10 +429,8 @@
             vmem((chunks, npl, 8, span), BF16),
             vmem((chunks, npl, 8, span), BF16),
             vmem((chunks, nz, 8, span), BF16),
-            vmem((chunks, 2, npl, 8, span), BF16),
             vmem((ng, nz, width), BF16),
             vmem((ng, nz, width), BF16),
-            vmem((nz, ng, width), BF16),
             vmem((nz, ng, width), BF16),
             dma((7,)),
             dma, dma((2,)),
@@ -460,18 +442,15 @@
             dma, dma((chunks,)),
             dma, dma,
             dma, dma,
-            dma,
         ]
+        in_vmem = pl.BlockSpec(memory_space=pltpu.VMEM)
         gx, grads = pl.pallas_call(
             functools.partial(kernel, dims, float(rows * rows) ** (-0.5)),
-            out_shape=(
-                jax.ShapeDtypeStruct((nz, ng, width), BF16),
-                jax.ShapeDtypeStruct((chunks, 2, npl, 8, span), BF16),
-            ),
+            out_shape=(vmem((nz, ng, width), BF16), vmem((chunks, 2, npl, 8, span), BF16)),
             in_specs=[pl.BlockSpec(memory_space=pl.ANY)] * 7,
-            out_specs=(pl.BlockSpec(memory_space=pl.ANY),) * 2,
+            out_specs=(in_vmem, in_vmem),
             scratch_shapes=scratch,
-            compiler_params=pltpu.CompilerParams(collective_id=0, has_side_effects=True, vmem_limit_bytes=62 * 2**20),
+            compiler_params=pltpu.CompilerParams(collective_id=0, has_side_effects=True, vmem_limit_bytes=60 * 2**20),
         )(saved_input.T, cotangent.T, w_in, bias_in, w_out, residual_logit, branch_scale)
         gxt, grad_in, grad_out = pl.pallas_call(
             finish,
@@ -480,14 +459,12 @@
                 jax.ShapeDtypeStruct((span, units), F32),
                 jax.ShapeDtypeStruct((units, span), F32),
             ),
-            in_specs=[pl.BlockSpec(memory_space=pl.ANY)] * 2,
+            in_specs=[in_vmem] * 2,
             out_specs=(pl.BlockSpec(memory_space=pl.ANY),) * 3,
             scratch_shapes=[
-                vmem(gx.shape, BF16), vmem(grads.shape, BF16),
-                vmem((width, rows), BF16), vmem((span, units), F32), vmem((units, span), F32),
-                dma((chunks + 1,)), dma((3,)),
+                vmem((width, rows), BF16), vmem((span, units), F32), vmem((units, span), F32), dma((3,)),
             ],
-            compiler_params=pltpu.CompilerParams(vmem_limit_bytes=62 * 2**20),
+            compiler_params=pltpu.CompilerParams(vmem_limit_bytes=48 * 2**20),
         )(gx, grads)
         return gxt.T, grad_in, grad_out
 

time: 60.7 us -> 57.7 us (0.951)
  Pallas kernels: 59.9 us -> 56.9 us
    pallas_call x1, Pallas kernels: 57.5 us -> 55.4 us  [step(): pl.pallas_call(functools.partial(kernel, dims, float(rows * rows) ** (-0....]
    pallas_call x1, Pallas kernels: 2.46 us -> 1.47 us  [step(): pl.pallas_call(finish, out_shape=(jax.ShapeDtypeStruct((width, rows), BF1...]
where the time goes in v5:
time: 57.7 us; the launch traced here: 57.5 us
  Pallas kernels  56.9 us (99%)
  between operations  0.64 us (1%)
    pallas_call x1, Pallas kernels, step(): pl.pallas_call(functools.partial(kernel, dims, float(rows * rows) ** (-0....  55.4 us
    pallas_call x1, Pallas kernels, step(): pl.pallas_call(finish, out_shape=(jax.ShapeDtypeStruct((width, rows), BF1...  1.47 us

profile of v5, /device:TPU:1, one launch (start us, length us, event | category | flops | bytes accessed | tf_op | source)
XLA Modules:
  0.0 57.5 jit_solution(7624982191896093169)
XLA Ops:
  0.6 55.4 %shard_map.94 = (bf16[8,32,192]{2,1,0:T(8,128)(2,1)S(1)}, bf16[6,2,16,8,384]{4,3,2,1,0:T(8,128)(2,1)S(1)}) custom-call(bf16[192,256]{1,0:T(8,128)(2,1)} %bitcast.3, bf16[192,256]{1,0:T(8,128)(2,1)} %bitcast.4, bf16[384,768]{1,0:T(8,128)(2,1)} %win_hbm.1, f32[768]{0:T(1024)} %bias_hbm.1, bf16[768,384]{1,0:T(8,128)(2,1)} %wout_hbm.1, f32[384]{0:T(512)} %logit_hbm.1, ...), custom_call_target="tpu_custom_call" | custom-call | tf_op jit(solution)/shard_map/pallas_call | solution.py:447
  56.1 1.5 %shard_map.95 = (bf16[192,256]{1,0:T(8,128)(2,1)}, f32[384,768]{1,0:T(8,128)}, f32[768,384]{1,0:T(8,128)}) custom-call(bf16[8,32,192]{2,1,0:T(8,128)(2,1)S(1)} %get-tuple-element.8.gx, bf16[6,2,16,8,384]{4,3,2,1,0:T(8,128)(2,1)S(1)} %get-tuple-element.9.grads), custom_call_target="tpu_custom_call" | custom-call | tf_op jit(solution)/shard_map/pallas_call | solution.py:455

commit v6 on v5

--- a/solution.py
+++ b/solution.py
@@ -97,13 +97,24 @@
     def greet(device):
         pl.semaphore_signal(barrier, inc=1, device_id=(device,), device_id_type=pl.DeviceIdType.MESH)
 
-    @pl.loop(1, nz)
-    def _(j):
-        greet(id_z(lax.rem(z + j, nz)))
-
-    @pl.loop(1, ng)
-    def _(j):
-        greet(id_group(lax.rem(group + j, ng)))
+    def hops(step, size):
+        return min(step, size - step)
+
+    z_steps = sorted(range(1, nz), key=lambda j: -hops(j, nz))
+    group_steps = [(jy, jx, jc) for jy in range(ny) for jx in range(nx) for jc in range(nc)][1:]
+    group_steps.sort(key=lambda j: -(hops(j[0], ny) + hops(j[1], nx)))
+    at_y, at_z, at_x, at_c = (
+        [lax.rem(here + j, size) if j else here for j in range(size)] for here, size in ((y, ny), (z, nz), (xc, nx), (c, nc))
+    )
+    id_y, id_x = [i * (nz * ns) for i in at_y], [i * nc for i in at_x]
+    group_y, own_z, own_group = [i * ns for i in at_y], z * ns, y * (nz * ns) + s
+    z_targets = [(at_z[j], at_z[j] * ns + own_group) for j in z_steps]
+    group_targets = []
+    for jy, jx, jc in group_steps:
+        in_plane = id_x[jx] + at_c[jc]
+        group_targets.append((group_y[jy] + in_plane, id_y[jy] + own_z + in_plane))
+    for _, device in z_targets + group_targets:
+        greet(device)
 
     operands = (
         (xt_hbm, xt.at[0]), (ct_hbm, xt.at[1]), (logit_hbm, logit_row), (scale_hbm, scale_row), (bias_hbm, bias_row),
@@ -182,8 +193,15 @@
 
         return each(count, copy, ref, recv_sem)
 
+    def exchange_with(targets, place, src, dst, send_sem, recv_sem):
+        def start():
+            for to, device in targets:
+                send(src.at[to], dst.at[place], send_sem, recv_sem, device).start()
+
+        return start, bytes_of(dst.at[pl.ds(0, len(targets))], recv_sem).wait
+
     def start_a(k):
-        start, wait = exchange(nz, z, xs.at[k], ra.at[k], a_send, a_recv.at[k], id_z)
+        start, wait = exchange_with(z_targets, z, xs.at[k], ra.at[k], a_send, a_recv.at[k])
         start()
         ra[k, z] = xs[k, z]
         return wait
@@ -195,7 +213,7 @@
         unfold(ra[k])
         for g in range(ng):
             tb[k, g] = strided(g, nz, ng)[:, :width].astype(BF16)
-        start, wait = exchange(ng, group, tb.at[k], rb.at[k], b_send, b_recv.at[k], id_group)
+        start, wait = exchange_with(group_targets, group, tb.at[k], rb.at[k], b_send, b_recv.at[k])
         start()
         rb[k, group] = tb[k, group]
         return wait

time: 57.7 us -> 56.5 us (0.979)
  Pallas kernels: 56.9 us -> 55.8 us
    pallas_call x1, Pallas kernels: 55.4 us -> 54.3 us  [step(): pl.pallas_call(functools.partial(kernel, dims, float(rows * rows) ** (-0....]
where the time goes in v6:
time: 56.5 us; the launch traced here: 56.4 us
  Pallas kernels  55.8 us (99%)
  between operations  0.64 us (1%)
    pallas_call x1, Pallas kernels, step(): pl.pallas_call(functools.partial(kernel, dims, float(rows * rows) ** (-0....  54.3 us
    pallas_call x1, Pallas kernels, step(): pl.pallas_call(finish, out_shape=(jax.ShapeDtypeStruct((width, rows), BF1...  1.47 us

profile of v6, /device:TPU:1, one launch (start us, length us, event | category | flops | bytes accessed | tf_op | source)
XLA Modules:
  0.0 56.4 jit_solution(7706997049592429078)
XLA Ops:
  0.6 54.3 %shard_map.94 = (bf16[8,32,192]{2,1,0:T(8,128)(2,1)S(1)}, bf16[6,2,16,8,384]{4,3,2,1,0:T(8,128)(2,1)S(1)}) custom-call(bf16[192,256]{1,0:T(8,128)(2,1)} %bitcast.3, bf16[192,256]{1,0:T(8,128)(2,1)} %bitcast.4, bf16[384,768]{1,0:T(8,128)(2,1)} %win_hbm.1, f32[768]{0:T(1024)} %bias_hbm.1, bf16[768,384]{1,0:T(8,128)(2,1)} %wout_hbm.1, f32[384]{0:T(512)} %logit_hbm.1, ...), custom_call_target="tpu_custom_call" | custom-call | tf_op jit(solution)/shard_map/pallas_call | solution.py:465
  55.0 1.5 %shard_map.95 = (bf16[192,256]{1,0:T(8,128)(2,1)}, f32[384,768]{1,0:T(8,128)}, f32[768,384]{1,0:T(8,128)}) custom-call(bf16[8,32,192]{2,1,0:T(8,128)(2,1)S(1)} %get-tuple-element.8.gx, bf16[6,2,16,8,384]{4,3,2,1,0:T(8,128)(2,1)S(1)} %get-tuple-element.9.grads), custom_call_target="tpu_custom_call" | custom-call | tf_op jit(solution)/shard_map/pallas_call | solution.py:473

commit v7 on v6

--- a/solution.py
+++ b/solution.py
@@ -81,9 +81,6 @@
     def id_of(zz, gg):
         return (lax.div(gg, ns) * nz + zz) * ns + lax.rem(gg, ns)
 
-    def id_plane(pp):
-        return ((lax.div(pp, nx) * nz + z) * nx + lax.rem(pp, nx)) * nc + c
-
     def id_z(zz):
         return id_of(zz, group)
 
@@ -113,6 +110,10 @@
     for jy, jx, jc in group_steps:
         in_plane = id_x[jx] + at_c[jc]
         group_targets.append((group_y[jy] + in_plane, id_y[jy] + own_z + in_plane))
+    plane_y = [i * nx for i in at_y]
+    plane_targets = [
+        (plane_y[jy] + at_x[jx], id_y[jy] + own_z + id_x[jx] + c) for jy, jx, jc in group_steps if jc == 0
+    ]
     for _, device in z_targets + group_targets:
         greet(device)
 
@@ -187,18 +188,19 @@
 
         return each(count, copy, dst, recv_sem)
 
-    def spread(count, place, ref, send_sem, recv_sem, device_of):
-        def copy(j):
-            return send(ref.at[place], ref.at[place], send_sem, recv_sem, device_of(lax.rem(place + j, count)))
-
-        return each(count, copy, ref, recv_sem)
-
     def exchange_with(targets, place, src, dst, send_sem, recv_sem):
         def start():
             for to, device in targets:
                 send(src.at[to], dst.at[place], send_sem, recv_sem, device).start()
 
         return start, bytes_of(dst.at[pl.ds(0, len(targets))], recv_sem).wait
+
+    def spread_with(targets, place, ref, send_sem, recv_sem):
+        def start():
+            for _, device in targets:
+                send(ref.at[place], ref.at[place], send_sem, recv_sem, device).start()
+
+        return start, bytes_of(ref.at[pl.ds(0, len(targets))], recv_sem).wait
 
     def start_a(k):
         start, wait = exchange_with(z_targets, z, xs.at[k], ra.at[k], a_send, a_recv.at[k])
@@ -284,7 +286,7 @@
     def start_d(k):
         to_sibling[k].wait_recv()
         hsum[k] = gb[k, c] + rc[k]
-        start, wait = exchange(npl, plane, hsum.at[k], rd.at[k], d_send, d_recv.at[k], id_plane)
+        start, wait = exchange_with(plane_targets, plane, hsum.at[k], rd.at[k], d_send, d_recv.at[k])
         start()
         plane_waits.append(wait)
         rd[k, plane] = hsum[k, plane]
@@ -339,7 +341,7 @@
     for k in range(chunks):
         plane_waits[k]()
         rz[k, z] = added(rd.at[k], npl).astype(BF16)
-        start, wait = spread(nz, z, rz.at[k], z_send, z_recv.at[k], id_z)
+        start, wait = spread_with(z_targets, z, rz.at[k], z_send, z_recv.at[k])
         start()
         z_waits.append(wait)
 
@@ -357,7 +359,7 @@
     for k in range(chunks):
         z_waits[k]()
         rg[k, c, plane] = (added(rz.at[k], nz) * scale_out).astype(BF16)
-        start, wait = spread(npl, plane, rg.at[k, c], e_send, e_recv.at[k], id_plane)
+        start, wait = spread_with(plane_targets, plane, rg.at[k, c], e_send, e_recv.at[k])
         start()
         gather_waits.append(wait)
         if k == chunks - 2:

time: 56.5 us -> 56 us (level)
  no operation moved by 1% of the time
where the time goes in v7:
time: 56 us; the launch traced here: 55.9 us
  Pallas kernels  55.3 us (99%)
  between operations  0.64 us (1%)
    pallas_call x1, Pallas kernels, step(): pl.pallas_call(functools.partial(kernel, dims, float(rows * rows) ** (-0....  53.8 us
    pallas_call x1, Pallas kernels, step(): pl.pallas_call(finish, out_shape=(jax.ShapeDtypeStruct((width, rows), BF1...  1.47 us

profile of v7, /device:TPU:1, one launch (start us, length us, event | category | flops | bytes accessed | tf_op | source)
XLA Modules:
  0.0 55.9 jit_solution(6780745529137523838)
XLA Ops:
  0.6 53.8 %shard_map.94 = (bf16[8,32,192]{2,1,0:T(8,128)(2,1)S(1)}, bf16[6,2,16,8,384]{4,3,2,1,0:T(8,128)(2,1)S(1)}) custom-call(bf16[192,256]{1,0:T(8,128)(2,1)} %bitcast.3, bf16[192,256]{1,0:T(8,128)(2,1)} %bitcast.4, bf16[384,768]{1,0:T(8,128)(2,1)} %win_hbm.1, f32[768]{0:T(1024)} %bias_hbm.1, bf16[768,384]{1,0:T(8,128)(2,1)} %wout_hbm.1, f32[384]{0:T(512)} %logit_hbm.1, ...), custom_call_target="tpu_custom_call" | custom-call | tf_op jit(solution)/shard_map/pallas_call | solution.py:467
  54.4 1.5 %shard_map.95 = (bf16[192,256]{1,0:T(8,128)(2,1)}, f32[384,768]{1,0:T(8,128)}, f32[768,384]{1,0:T(8,128)}) custom-call(bf16[8,32,192]{2,1,0:T(8,128)(2,1)S(1)} %get-tuple-element.8.gx, bf16[6,2,16,8,384]{4,3,2,1,0:T(8,128)(2,1)S(1)} %get-tuple-element.9.grads), custom_call_target="tpu_custom_call" | custom-call | tf_op jit(solution)/shard_map/pallas_call | solution.py:475
